TPU v7x, 512 devices: a whole 4x8x8 slice. The times are simulated.
512 devices in a mesh: dp: 32 (over z_hi, y), space: 16 (over x, z_lo, core).
Axes of the slice: x: 4, y: 8, z: 8 (z_hi: 4, z_lo: 2; z = z_hi * 2 + z_lo), core: 2. Of those that a mesh axis runs over, the one named last changes fastest.
Arguments:
- activations: bfloat16 [32, 64, 32, 48, 128], P('dp', None, 'space'), may hold values from -6 to 6
- cotangent: bfloat16 [32, 64, 32, 48, 128], P('dp', None, 'space'), may hold values from -6 to 6
- mode_weights: bfloat16 [2048, 64, 128], P(('space', 'dp')), may hold values from -6 to 6
- pointwise: bfloat16 [64, 64], replicated, may hold values from -0.75 to 0.75
- offsets: float32 [64], replicated, may hold values from -3 to 3
Outputs:
- grad_in: bfloat16 [32, 64, 32, 48, 128], P('dp', None, 'space')
- grad_spectral: float32 [2048, 64, 128], P(('space', 'dp'))
All inputs are finite; a program needn't handle non-finite values.
Results may differ from a plain program's by a relative error of at most 0.02.
Values may be sent and summed in bfloat16 or wider, within the bound.
A program may use at most 64 MiB of HBM per device.

v0:
```python
import math

import jax
import jax.numpy as jnp
from jax import lax
from jax.sharding import PartitionSpec as P

MX = 16
MY = 16
MZ = 8
NX = 32


def centered(count):
    index = jnp.arange(count, dtype=jnp.int32)
    return jnp.where(index < count // 2, index, index - count)


def plane_tables(rows_y, rows_z, modes_y, modes_z):
    along_y = jnp.arange(rows_y, dtype=jnp.int32)[:, None, None, None]
    along_z = jnp.arange(rows_z, dtype=jnp.int32)[None, :, None, None]
    freq_y = centered(modes_y)[None, None, :, None]
    freq_z = jnp.arange(modes_z, dtype=jnp.int32)[None, None, None, :]
    phase = jnp.mod(freq_y * along_y * rows_z + freq_z * along_z * rows_y, rows_y * rows_z)
    theta = phase.astype(jnp.float32) * (2.0 * math.pi / (rows_y * rows_z))
    cosine = jnp.cos(theta)
    sine = jnp.sin(theta)
    forward = jnp.stack([cosine, -sine], -1).reshape(rows_y * rows_z, modes_y * modes_z * 2)
    scaled = jnp.where(freq_z == 0, 1.0, 2.0).astype(jnp.float32) / (rows_y * rows_z)
    inverse = (
        jnp.stack([cosine * scaled, -sine * scaled], -1)
        .reshape(rows_y * rows_z, modes_y * modes_z * 2)
        .T
    )
    return (forward.astype(jnp.bfloat16), inverse.astype(jnp.bfloat16))


def line_tables(length, modes):
    along = jnp.arange(length, dtype=jnp.int32)[:, None]
    freq = centered(modes)[None, :]
    phase = jnp.mod(freq * along, length)
    theta = phase.astype(jnp.float32) * (2.0 * math.pi / length)
    cosine = jnp.cos(theta)
    sine = jnp.sin(theta)
    first = jnp.stack([cosine, -sine], -1)
    second = jnp.stack([sine, cosine], -1)
    forward = jnp.stack([first, second], 1).reshape(2 * length, 2 * modes)
    inv_first = jnp.stack([cosine.T, sine.T], -1) / length
    inv_second = jnp.stack([-sine.T, cosine.T], -1) / length
    inverse = jnp.stack([inv_first, inv_second], 1).reshape(2 * modes, 2 * length)
    return (forward.astype(jnp.bfloat16), inverse.astype(jnp.bfloat16))


def expand_weights(weights):
    half = weights.shape[1]
    real_part = weights[:, :, :half]
    imag_part = weights[:, :, half:]
    upper = jnp.concatenate([real_part, imag_part], axis=2)
    lower = jnp.concatenate([-imag_part, real_part], axis=2)
    return jnp.concatenate([upper, lower], axis=1)


def outer_sum(left, right):
    return jnp.einsum("mbi,mbo->mio", left, right, preferred_element_type=jnp.float32)


def weight_terms(spec_in, spec_grad):
    half = spec_in.shape[2] // 2
    in_real = spec_in[:, :, :half]
    in_imag = spec_in[:, :, half:]
    gr_real = spec_grad[:, :, :half]
    gr_imag = spec_grad[:, :, half:]
    real_term = outer_sum(in_real, gr_real) + outer_sum(in_imag, gr_imag)
    imag_term = outer_sum(in_real, gr_imag) - outer_sum(in_imag, gr_real)
    return jnp.concatenate([real_term, imag_term], axis=2)


def to_modes(slab, table, modes_x):
    samples, channels, width, pairs = slab.shape
    moved = lax.all_to_all(slab, "space", split_axis=3, concat_axis=2, tiled=True)
    length = moved.shape[2]
    local = moved.shape[3] // 2
    lines = moved.reshape(samples, channels, length, local, 2).transpose(0, 1, 3, 2, 4)
    lines = lines.reshape(samples, channels, local, 2 * length)
    spectra = jnp.dot(lines, table, preferred_element_type=jnp.float32).astype(jnp.bfloat16)
    spectra = spectra.reshape(samples, channels, local, modes_x, 2).transpose(2, 3, 0, 4, 1)
    return spectra.reshape(local * modes_x, samples, 2 * channels)


def to_slab(spectra, table, modes_x, channels):
    count, samples, doubled = spectra.shape
    local = count // modes_x
    lines = spectra.reshape(local, modes_x, samples, 2, channels).transpose(2, 4, 0, 1, 3)
    lines = lines.reshape(samples, channels, local, 2 * modes_x)
    lines = jnp.dot(lines, table, preferred_element_type=jnp.float32).astype(jnp.bfloat16)
    length = lines.shape[3] // 2
    lines = lines.reshape(samples, channels, local, length, 2).transpose(0, 1, 3, 2, 4)
    lines = lines.reshape(samples, channels, length, 2 * local)
    return lax.all_to_all(lines, "space", split_axis=2, concat_axis=3, tiled=True)


def to_owners(spectra):
    return lax.all_to_all(spectra, "dp", split_axis=0, concat_axis=1, tiled=True)


def from_owners(spectra):
    return lax.all_to_all(spectra, "dp", split_axis=1, concat_axis=0, tiled=True)


def gelu_slope(value):
    cdf = 0.5 * (1.0 + lax.erf(value * 0.7071067811865476))
    density = jnp.exp(-0.5 * value * value) * 0.3989422804014327
    return cdf + value * density


def body(activations, cotangent, mode_weights, pointwise, offsets):
    samples, channels, width, rows_y, rows_z = activations.shape
    plane_fwd, plane_inv = plane_tables(rows_y, rows_z, MY, MZ)
    line_fwd, line_inv = line_tables(NX, MX)
    flat = activations.reshape(samples, channels, width, rows_y * rows_z)
    planes = jnp.dot(flat, plane_fwd, preferred_element_type=jnp.float32).astype(jnp.bfloat16)
    spec_in = to_modes(planes, line_fwd, MX)
    blocks = expand_weights(mode_weights)
    held_in = to_owners(spec_in)
    held_out = jnp.einsum(
        "mbi,mio->mbo", held_in, blocks, preferred_element_type=jnp.float32
    ).astype(jnp.bfloat16)
    spec_out = from_owners(held_out)
    returned = to_slab(spec_out, line_inv, MX, channels)
    spectral = jnp.dot(returned, plane_inv, preferred_element_type=jnp.float32)
    local_part = jnp.einsum("io,bixn->boxn", pointwise, flat, preferred_element_type=jnp.float32)
    summed = spectral + local_part + offsets[None, :, None, None]
    upstream = cotangent.reshape(flat.shape).astype(jnp.float32)
    slope_grad = (upstream * gelu_slope(summed)).astype(jnp.bfloat16)
    back_plane = jnp.dot(slope_grad, plane_inv.T, preferred_element_type=jnp.float32).astype(
        jnp.bfloat16
    )
    spec_grad = to_modes(back_plane, line_inv.T, MX)
    held_grad = to_owners(spec_grad)
    held_dx = jnp.einsum(
        "mbo,mio->mbi", held_grad, blocks, preferred_element_type=jnp.float32
    ).astype(jnp.bfloat16)
    spec_dx = from_owners(held_dx)
    grad_spectral = weight_terms(held_in, held_grad)
    line_dx = to_slab(spec_dx, line_fwd.T, MX, channels)
    total = jnp.dot(line_dx, plane_fwd.T, preferred_element_type=jnp.float32)
    total = total + jnp.einsum(
        "io,boxn->bixn", pointwise, slope_grad, preferred_element_type=jnp.float32
    )
    grad_in = total.astype(jnp.bfloat16).reshape(activations.shape)
    return (grad_in, grad_spectral)


def solution(mesh):
    return jax.shard_map(
        body,
        mesh=mesh,
        in_specs=(
            P("dp", None, "space", None, None),
            P("dp", None, "space", None, None),
            P(("space", "dp"), None, None),
            P(),
            P(),
        ),
        out_specs=(P("dp", None, "space", None, None), P(("space", "dp"), None, None)),
        check_vma=False,
    )
```

profile of v0, /device:TPU:1, one launch (start us, length us, event | category | flops | bytes accessed | tf_op | source)
XLA Modules:
  0.0 175.4 jit_solution(9613062227627259617)
XLA Ops:
  0.8 3.5 %reshape.620 = bf16[64,2,6144]{2,1,0:T(2,128)(2,1)S(1)} reshape(bf16[1,64,2,48,128]{4,3,2,1,0:T(8,128)(2,1)} %param.5) | data formatting | bytes 3145728 | tf_op jit(solution)/shard_map/reshape.4
  4.2 13.7 %multiply_convert_fusion.1 = (bf16[48,128,16,8,1]{1,0,4,3,2:T(8,128)(2,1)S(1)}, bf16[48,128,16,8,1]{1,0,4,3,2:T(8,128)(2,1)S(1)}, bf16[48,128,16,8,1]{1,0,4,3,2:T(8,128)(2,1)S(1)}, bf16[48,128,16,8,1]{1,0,4,3,2:T(8,128)(2,1)S(1)}) fusion(f32[8]{0:T(128)S(1)} %fusion.67, s32[128,8]{0,1:T(8,128)S(1)} %multiply_multiply_fusion.2, ...), kind=kLoop, calls=%fused_computation.26 | loop fusion | flops 12582912 | bytes 6298656 | tf_op jit(solution)/shard_map/convert.1
  17.9 2.0 %pad_maximum_fusion = (bf16[48,128,16,8,2]{1,0,4,3,2:T(8,128)(2,1)S(1)}, bf16[48,128,16,8,2]{1,0,4,3,2:T(8,128)(2,1)}) fusion(bf16[48,128,16,8,1]{1,0,4,3,2:T(8,128)(2,1)S(1)} %get-tuple-element.14, bf16[48,128,16,8,1]{1,0,4,3,2:T(8,128)(2,1)S(1)} %get-tuple-element.15, bf16[48,128,16,8,1]{1,0,4,3,2:T(8,128)(2,1)S(1)} %get-tuple-element.13, ...), kind=kLoop, calls=%fused_computation.22 | loop fusion | flops 3145728 | bytes 12582912 | tf_op jit(solution)/shard_map/stack | solution.py:28
  19.9 1.6 copy-done.1
  21.5 1.2 fusion.32
  23.6 10.2 %all-to-all-start = ((bf16[16,2,1024]{2,1,0:T(2,128)(2,1)}), bf16[16,2,1024]{2,1,0:T(2,128)(2,1)S(1)}, u32[]{:S(2)}, u32[]{:S(2)}) async-start(bf16[16,2,1024]{2,1,0:T(2,128)(2,1)} %reshape.655), calls=%async_computation | async-start | bytes 131072 | tf_op jit(solution)/shard_map/all_to_all | solution.py:80
  36.6 1.4 fusion.64
  38.0 1.6 all-to-all-done
  42.8 12.2 %all-to-all-start.1 = ((bf16[32,2,256]{2,1,0:T(2,128)(2,1)}), bf16[32,2,256]{2,1,0:T(2,128)(2,1)S(1)}, u32[]{:S(2)}, u32[]{:S(2)}) async-start(bf16[32,2,256]{2,1,0:T(2,128)(2,1)} %reshape.657), calls=%async_computation.1 | async-start | bytes 65536 | tf_op jit(solution)/shard_map/all_to_all | solution.py:103
  55.8 10.4 %all-to-all-done.1 = bf16[32,2,256]{2,1,0:T(2,128)(2,1)S(1)} async-done(((bf16[32,2,256]{2,1,0:T(2,128)(2,1)}), bf16[32,2,256]{2,1,0:T(2,128)(2,1)S(1)}, u32[]{:S(2)}, u32[]{:S(2)}) %all-to-all-start.1) | async-done | bytes 32800 | tf_op jit(solution)/shard_map/all_to_all | solution.py:103
  67.1 3.9 %all-to-all-start.2 = ((bf16[4,32,128]{2,0,1:T(4,128)(2,1)}), bf16[4,32,128]{2,0,1:T(4,128)(2,1)S(1)}, u32[]{:S(2)}, u32[]{:S(2)}) async-start(bf16[4,32,128]{2,0,1:T(4,128)(2,1)} %copy.95), calls=%async_computation.2 | async-start | bytes 65536 | tf_op jit(solution)/shard_map/all_to_all | solution.py:107
  73.5 2.9 %reshape.650 = f32[1,64,2,6144]{3,2,1,0:T(2,128)} reshape(bf16[1,64,2,48,128]{4,3,2,1,0:T(8,128)(2,1)S(1)} %copy-done.3) | data formatting | bytes 4718592 | tf_op jit(solution)/shard_map/convert_element_type | solution.py:133
  76.4 5.6 %all-to-all-done.2 = bf16[4,32,128]{2,0,1:T(4,128)(2,1)S(1)} async-done(((bf16[4,32,128]{2,0,1:T(4,128)(2,1)}), bf16[4,32,128]{2,0,1:T(4,128)(2,1)S(1)}, u32[]{:S(2)}, u32[]{:S(2)}) %all-to-all-start.2) | async-done | bytes 32800 | tf_op jit(solution)/shard_map/all_to_all | solution.py:107
  83.4 6.7 %all-to-all-start.3 = ((bf16[16,2,1024]{2,1,0:T(2,128)(2,1)}), bf16[16,2,1024]{2,1,0:T(2,128)(2,1)S(1)}, u32[]{:S(2)}, u32[]{:S(2)}) async-start(bf16[16,2,1024]{2,1,0:T(2,128)(2,1)} %reshape.659), calls=%async_computation.3 | async-start | bytes 131072 | tf_op jit(solution)/shard_map/all_to_all | solution.py:99
  90.1 2.4 %convolution_bitcast_fusion.1 = f32[1,64,2,6144]{3,1,2,0:T(8,128)} fusion(bf16[64,2,6144]{2,1,0:T(2,128)(2,1)S(1)} %reshape.620, bf16[64,64]{1,0:T(8,128)(2,1)S(1)} %copy-done), kind=kOutput, calls=%fused_computation.1 | convolution fusion | flops 100663296 | bytes 4726784 | tf_op jit(solution)/shard_map/io,bixn->boxn/dot_general | solution.py:131
  92.4 3.4 %all-to-all-done.3 = bf16[16,2,1024]{2,1,0:T(2,128)(2,1)S(1)} async-done(((bf16[16,2,1024]{2,1,0:T(2,128)(2,1)}), bf16[16,2,1024]{2,1,0:T(2,128)(2,1)S(1)}, u32[]{:S(2)}, u32[]{:S(2)}) %all-to-all-start.3) | async-done | bytes 65568 | tf_op jit(solution)/shard_map/all_to_all | solution.py:99
  96.1 7.0 %fusion.14 = bf16[64,2,6144]{2,0,1:T(8,128)(2,1)S(1)} fusion(f32[1,64,2,6144]{3,1,2,0:T(8,128)} %convolution_bitcast_fusion.1, bf16[64,2,256]{0,2,1:T(8,128)(2,1)S(1)} %bitcast.250, f32[1,64,2,6144]{3,2,1,0:T(2,128)} %reshape.650, bf16[32,8,48,128]{3,2,1,0:T(8,128)(2,1)} %bitcast.211, f32[64]{0:T(128)S(1)} %copy-done.13), kind=kOutput, calls=%fused_computation.24 | convolution fusion | flops 412090368 | bytes 11075840 | tf_op jit(solution)/shard_map/dot_general | solution.py:130
  104.2 1.2 fusion.31
  106.3 3.7 %all-to-all-start.4 = ((bf16[16,2,1024]{2,1,0:T(2,128)(2,1)}), bf16[16,2,1024]{2,1,0:T(2,128)(2,1)S(1)}, u32[]{:S(2)}, u32[]{:S(2)}) async-start(bf16[16,2,1024]{2,1,0:T(2,128)(2,1)} %reshape.661), calls=%async_computation.4 | async-start | bytes 131072 | tf_op jit(solution)/shard_map/all_to_all | solution.py:80
  110.1 5.9 %all-to-all-done.4 = bf16[16,2,1024]{2,1,0:T(2,128)(2,1)S(1)} async-done(((bf16[16,2,1024]{2,1,0:T(2,128)(2,1)}), bf16[16,2,1024]{2,1,0:T(2,128)(2,1)S(1)}, u32[]{:S(2)}, u32[]{:S(2)}) %all-to-all-start.4) | async-done | bytes 65568 | tf_op jit(solution)/shard_map/all_to_all | solution.py:80
  117.9 5.1 %all-to-all-start.5 = ((bf16[32,2,256]{2,1,0:T(2,128)(2,1)}), bf16[32,2,256]{2,1,0:T(2,128)(2,1)S(1)}, u32[]{:S(2)}, u32[]{:S(2)}) async-start(bf16[32,2,256]{2,1,0:T(2,128)(2,1)} %reshape.663), calls=%async_computation.5 | async-start | bytes 65536 | tf_op jit(solution)/shard_map/all_to_all | solution.py:103
  123.0 2.0 %convolution_bitcast_fusion = f32[1,64,2,6144]{3,1,2,0:T(8,128)S(1)} fusion(bf16[64,2,6144]{2,0,1:T(8,128)(2,1)} %copy-done.4, bf16[64,64]{1,0:T(8,128)(2,1)S(1)} %copy-done), kind=kOutput, calls=%fused_computation | convolution fusion | flops 100663296 | bytes 4726784 | tf_op jit(solution)/shard_map/io,boxn->bixn/dot_general | solution.py:147
  125.0 9.2 %all-to-all-done.5 = bf16[32,2,256]{2,1,0:T(2,128)(2,1)S(1)} async-done(((bf16[32,2,256]{2,1,0:T(2,128)(2,1)}), bf16[32,2,256]{2,1,0:T(2,128)(2,1)S(1)}, u32[]{:S(2)}, u32[]{:S(2)}) %all-to-all-start.5) | async-done | bytes 32800 | tf_op jit(solution)/shard_map/all_to_all | solution.py:103
  135.6 3.9 %all-to-all-start.6 = ((bf16[4,32,128]{2,0,1:T(4,128)(2,1)}), bf16[4,32,128]{2,0,1:T(4,128)(2,1)S(1)}, u32[]{:S(2)}, u32[]{:S(2)}) async-start(bf16[4,32,128]{2,0,1:T(4,128)(2,1)} %copy.113), calls=%async_computation.6 | async-start | bytes 65536 | tf_op jit(solution)/shard_map/all_to_all | solution.py:107
  139.7 10.9 %all-to-all-done.6 = bf16[4,32,128]{2,0,1:T(4,128)(2,1)S(1)} async-done(((bf16[4,32,128]{2,0,1:T(4,128)(2,1)}), bf16[4,32,128]{2,0,1:T(4,128)(2,1)S(1)}, u32[]{:S(2)}, u32[]{:S(2)}) %all-to-all-start.6) | async-done | bytes 32800 | tf_op jit(solution)/shard_map/all_to_all | solution.py:107
  152.1 1.6 convolution_convert_fusion
  153.6 1.7 copy.114
  157.0 1.7 reshape.665
  158.6 6.3 %all-to-all-start.7 = ((bf16[16,2,1024]{2,1,0:T(2,128)(2,1)}), bf16[16,2,1024]{2,1,0:T(2,128)(2,1)S(1)}, u32[]{:S(2)}, u32[]{:S(2)}) async-start(bf16[16,2,1024]{2,1,0:T(2,128)(2,1)} %reshape.665), calls=%async_computation.7 | async-start | bytes 131072 | tf_op jit(solution)/shard_map/all_to_all | solution.py:99
  166.0 4.8 %all-to-all-done.7 = bf16[16,2,1024]{2,1,0:T(2,128)(2,1)S(1)} async-done(((bf16[16,2,1024]{2,1,0:T(2,128)(2,1)}), bf16[16,2,1024]{2,1,0:T(2,128)(2,1)S(1)}, u32[]{:S(2)}, u32[]{:S(2)}) %all-to-all-start.7) | async-done | bytes 65568 | tf_op jit(solution)/shard_map/all_to_all | solution.py:99
  171.0 2.8 %fusion.3 = bf16[1,64,2,6144]{3,1,2,0:T(8,128)(2,1)S(1)} fusion(f32[1,64,2,6144]{3,1,2,0:T(8,128)S(1)} %convolution_bitcast_fusion, bf16[64,2,256]{0,2,1:T(8,128)(2,1)S(1)} %bitcast.221, bf16[32,8,48,128]{3,2,1,0:T(8,128)(2,1)} %bitcast.208), kind=kOutput, calls=%fused_computation.7 | convolution fusion | flops 404226048 | bytes 7929856 | tf_op jit(solution)/shard_map/dot_general | solution.py:146
  174.1 1.3 copy.120
  (91 shorter events, 22.8 us)
Async XLA Ops:
  0.6 89.4 %copy-start = (bf16[64,64]{1,0:T(8,128)(2,1)S(1)}, bf16[64,64]{1,0:T(8,128)(2,1)}, u32[]{:S(2)}) copy-start(bf16[64,64]{1,0:T(8,128)(2,1)} %param.8) | copy-start | bytes 24580
  0.7 33.1 %copy-start.12 = (s32[16]{0:T(128)}, s32[16]{0:T(128)S(1)}, u32[]{:S(2)}) copy-start(s32[16]{0:T(128)S(1)} %compare_select_fusion) | copy-start | bytes 196
  19.9 1.6 copy-start.1
  21.5 15.0 %copy-start.5 = (bf16[4,64,128]{2,1,0:T(8,128)(2,1)S(1)}, bf16[4,64,128]{2,1,0:T(8,128)(2,1)}, u32[]{:S(2)}) copy-start(bf16[4,64,128]{2,1,0:T(8,128)(2,1)} %param.7) | copy-start | bytes 196612
  22.7 50.8 %copy-start.3 = (bf16[1,64,2,48,128]{4,3,2,1,0:T(8,128)(2,1)S(1)}, bf16[1,64,2,48,128]{4,3,2,1,0:T(8,128)(2,1)}, u32[]{:S(2)}) copy-start(bf16[1,64,2,48,128]{4,3,2,1,0:T(8,128)(2,1)} %param.6) | copy-start | bytes 4718596
  23.6 16.1 %all-to-all-start = ((bf16[16,2,1024]{2,1,0:T(2,128)(2,1)}), bf16[16,2,1024]{2,1,0:T(2,128)(2,1)S(1)}, u32[]{:S(2)}, u32[]{:S(2)}) async-start(bf16[16,2,1024]{2,1,0:T(2,128)(2,1)} %reshape.655), calls=%async_computation | async-start | bytes 131072 | tf_op jit(solution)/shard_map/all_to_all | solution.py:80
  36.6 34.4 %copy-start.8 = (bf16[4,64,64]{2,1,0:T(8,128)(2,1)}, bf16[4,64,64]{2,1,0:T(8,128)(2,1)S(1)}, u32[]{:S(2)}) copy-start(bf16[4,64,64]{2,1,0:T(8,128)(2,1)S(1)} %get-tuple-element.10) | copy-start | bytes 98308
  36.6 34.4 %copy-start.10 = (bf16[4,64,64]{2,1,0:T(8,128)(2,1)}, bf16[4,64,64]{2,1,0:T(8,128)(2,1)S(1)}, u32[]{:S(2)}) copy-start(bf16[4,64,64]{2,1,0:T(8,128)(2,1)S(1)} %get-tuple-element.11) | copy-start | bytes 98308
  42.8 23.4 %all-to-all-start.1 = ((bf16[32,2,256]{2,1,0:T(2,128)(2,1)}), bf16[32,2,256]{2,1,0:T(2,128)(2,1)S(1)}, u32[]{:S(2)}, u32[]{:S(2)}) async-start(bf16[32,2,256]{2,1,0:T(2,128)(2,1)} %reshape.657), calls=%async_computation.1 | async-start | bytes 65536 | tf_op jit(solution)/shard_map/all_to_all | solution.py:103
  67.1 15.0 %all-to-all-start.2 = ((bf16[4,32,128]{2,0,1:T(4,128)(2,1)}), bf16[4,32,128]{2,0,1:T(4,128)(2,1)S(1)}, u32[]{:S(2)}, u32[]{:S(2)}) async-start(bf16[4,32,128]{2,0,1:T(4,128)(2,1)} %copy.95), calls=%async_computation.2 | async-start | bytes 65536 | tf_op jit(solution)/shard_map/all_to_all | solution.py:107
  73.5 8.6 %copy-start.7 = (bf16[32,64,1]{1,0,2:T(8,128)(2,1)S(1)}, bf16[32,64,1]{1,0,2:T(8,128)(2,1)}, u32[]{:S(2)}) copy-start(bf16[32,64,1]{1,0,2:T(8,128)(2,1)} %reshape.644) | copy-start | bytes 12292
  82.4 13.7 %copy-start.13 = (f32[64]{0:T(128)S(1)}, f32[64]{0:T(128)}, u32[]{:S(2)}) copy-start(f32[64]{0:T(128)} %param.9) | copy-start | bytes 772
  83.4 12.5 %all-to-all-start.3 = ((bf16[16,2,1024]{2,1,0:T(2,128)(2,1)}), bf16[16,2,1024]{2,1,0:T(2,128)(2,1)S(1)}, u32[]{:S(2)}, u32[]{:S(2)}) async-start(bf16[16,2,1024]{2,1,0:T(2,128)(2,1)} %reshape.659), calls=%async_computation.3 | async-start | bytes 131072 | tf_op jit(solution)/shard_map/all_to_all | solution.py:99
  96.1 8.2 %copy-start.2 = (bf16[48,128,16,8,2]{1,0,4,3,2:T(8,128)(2,1)S(1)}, bf16[48,128,16,8,2]{1,0,4,3,2:T(8,128)(2,1)}, u32[]{:S(2)}) copy-start(bf16[48,128,16,8,2]{1,0,4,3,2:T(8,128)(2,1)} %get-tuple-element.27) | copy-start | bytes 9437188
  103.1 1.1 copy-start.4
  106.3 9.6 %all-to-all-start.4 = ((bf16[16,2,1024]{2,1,0:T(2,128)(2,1)}), bf16[16,2,1024]{2,1,0:T(2,128)(2,1)S(1)}, u32[]{:S(2)}, u32[]{:S(2)}) async-start(bf16[16,2,1024]{2,1,0:T(2,128)(2,1)} %reshape.661), calls=%async_computation.4 | async-start | bytes 131072 | tf_op jit(solution)/shard_map/all_to_all | solution.py:80
  116.1 18.2 %copy-start.9 = (bf16[4,64,64]{2,1,0:T(8,128)(2,1)S(1)}, bf16[4,64,64]{2,1,0:T(8,128)(2,1)}, u32[]{:S(2)}) copy-start(bf16[4,64,64]{2,1,0:T(8,128)(2,1)} %copy-done.8) | copy-start | bytes 98308
  116.1 18.2 %copy-start.11 = (bf16[4,64,64]{2,1,0:T(8,128)(2,1)S(1)}, bf16[4,64,64]{2,1,0:T(8,128)(2,1)}, u32[]{:S(2)}) copy-start(bf16[4,64,64]{2,1,0:T(8,128)(2,1)} %copy-done.10) | copy-start | bytes 98308
  117.9 16.3 %all-to-all-start.5 = ((bf16[32,2,256]{2,1,0:T(2,128)(2,1)}), bf16[32,2,256]{2,1,0:T(2,128)(2,1)S(1)}, u32[]{:S(2)}, u32[]{:S(2)}) async-start(bf16[32,2,256]{2,1,0:T(2,128)(2,1)} %reshape.663), calls=%async_computation.5 | async-start | bytes 65536 | tf_op jit(solution)/shard_map/all_to_all | solution.py:103
  135.6 15.0 %all-to-all-start.6 = ((bf16[4,32,128]{2,0,1:T(4,128)(2,1)}), bf16[4,32,128]{2,0,1:T(4,128)(2,1)S(1)}, u32[]{:S(2)}, u32[]{:S(2)}) async-start(bf16[4,32,128]{2,0,1:T(4,128)(2,1)} %copy.113), calls=%async_computation.6 | async-start | bytes 65536 | tf_op jit(solution)/shard_map/all_to_all | solution.py:107
  150.6 0.6 copy-start.6
  158.6 12.1 %all-to-all-start.7 = ((bf16[16,2,1024]{2,1,0:T(2,128)(2,1)}), bf16[16,2,1024]{2,1,0:T(2,128)(2,1)S(1)}, u32[]{:S(2)}, u32[]{:S(2)}) async-start(bf16[16,2,1024]{2,1,0:T(2,128)(2,1)} %reshape.665), calls=%async_computation.7 | async-start | bytes 131072 | tf_op jit(solution)/shard_map/all_to_all | solution.py:99
where the time goes:
time: 176 us; the launch traced here: 175 us
  starting transfers between devices  51.9 us (29%)
  waiting for transfers between devices  51.9 us (29%)
  local copies, waits for them, and re-layouts  28.1 us (16%)
  other arithmetic  21.8 us (12%)
  matrix products  20.7 us (12%)
    all_to_all x2, waiting for transfers between devices, to_owners(): lax.all_to_all(spectra, 'dp', split_axis=0, concat_axis=1, tiled=True)  19.6 us
    all_to_all x2, starting transfers between devices, to_owners(): lax.all_to_all(spectra, 'dp', split_axis=0, concat_axis=1, tiled=True)  17.3 us
    all_to_all x2, waiting for transfers between devices, from_owners(): lax.all_to_all(spectra, 'dp', split_axis=1, concat_axis=0, tiled=True)  16.5 us
    another operation x3, other arithmetic  14.6 us
    all_to_all x2, starting transfers between devices, to_modes(): lax.all_to_all(slab, 'space', split_axis=3, concat_axis=2, tiled=True)  13.9 us
    all_to_all x2, starting transfers between devices, to_slab(): lax.all_to_all(lines, 'space', split_axis=2, concat_axis=3, tiled=True)  12.9 us
    unnamed x44, local copies, waits for them, and re-layouts  11 us
    all_to_all x2, waiting for transfers between devices, to_slab(): lax.all_to_all(lines, 'space', split_axis=2, concat_axis=3, tiled=True)  8.27 us
  transfers between devices with their start and end apart: 8, of which 8 were waited for; matrix products, arithmetic and copies ran while one was open for 9% of the time, Pallas kernels for 0%

commit v1 on v0

v1 whole, which is shorter than its diff:
```python
import jax
import jax.numpy as jnp
import numpy as np
from jax import lax
from jax.experimental import pallas as pl
from jax.experimental.pallas import tpu as pltpu
from jax.sharding import PartitionSpec as P

MX, MY, MZ = 16, 16, 8
NX, NY, NZ = 32, 48, 128
C = 64
GRP = 8
MESH = pl.DeviceIdType.MESH
F32, BF16 = jnp.float32, jnp.bfloat16


def centered(count):
    index = np.arange(count)
    return np.where(index < count // 2, index, index - count)


def tables():
    ty = 2 * np.pi * centered(MY)[:, None] * np.arange(NY)[None, :] / NY
    along_y = np.stack([np.cos(ty), -np.sin(ty)], 1)
    eye = np.eye(GRP)
    to_y = np.einsum("jry,cd->jrcdy", along_y, eye).reshape(MY * 2 * GRP, GRP * NY)
    tz = 2 * np.pi * np.arange(MZ)[:, None] * np.arange(NZ)[None, :] / NZ
    along_z = np.zeros((MZ, 2, 2, NZ))
    along_z[:, 0, 0], along_z[:, 0, 1] = np.cos(tz), np.sin(tz)
    along_z[:, 1, 0], along_z[:, 1, 1] = -np.sin(tz), np.cos(tz)
    weight = np.where(np.arange(MZ) == 0, 1.0, 2.0)[:, None, None, None]
    plain = along_z.reshape(MZ * 2, 2 * NZ)
    weighted = (along_z * weight).reshape(MZ * 2, 2 * NZ)
    s = 2 * np.pi * centered(MX)[None, :] * np.arange(NX)[:, None] / NX
    line = np.zeros((NX, 2, MX, 2))
    line[:, 0, :, 0], line[:, 0, :, 1] = np.cos(s), -np.sin(s)
    line[:, 1, :, 0], line[:, 1, :, 1] = np.sin(s), np.cos(s)
    line = line.reshape(NX // 2, 2, 2, MX, 2)
    to_q = np.einsum("shuqa,bd,ke->hakqbdseu", line, np.eye(4), np.eye(2)).reshape(512, 256)
    to_x = np.einsum("shuqa,bd,ke->habskueqd", line, np.eye(4), np.eye(2)).reshape(1024, 128)
    cast = lambda t: np.asarray(t.astype(np.float32)).astype(jnp.bfloat16)
    return tuple(cast(t) for t in (to_y, to_y.T.copy(), plain, weighted, to_q, to_x))


def dot(a, b, dims=((1,), (0,))):
    return lax.dot_general(a, b, (dims, ((), ())), preferred_element_type=F32)


def gelu_slope(value):
    cdf = 0.5 * (1.0 + lax.erf(value * 0.7071067811865476))
    density = jnp.exp(-0.5 * value * value) * 0.3989422804014327
    return cdf + value * density


def kernel(
    act_h, cot_h, w_h, pw_ref, off_ref, by_h, byt_h, fz_h, fzw_h, bq_h, bx_h,
    out_h, gs_h,
    act, cot, w_own, by, byt, fz, fzw, bq, bx,
    mid, loc, slope, outb, offb, kron, wall, wbuf, spec, xin, din, gsb,
    send, back, land,
    in_sem, tab_sem, w_sem, out_sem, ssem, rsem, wssem, wrsem, xssem, xrsem,
):
    dp = lax.axis_index("dp")
    s = lax.axis_index("space")
    zh, y = dp // 8, dp % 8
    me = zh * 16 + s
    low = lax.broadcasted_iota(jnp.int32, (1, 128), 1) < 64

    def at(tt):
        return ((tt // 16) * 8 + y, tt % 16)

    bar = pltpu.get_barrier_semaphore()

    def hello(t, c):
        pl.semaphore_signal(bar, inc=1, device_id=at((me + t) % 64), device_id_type=MESH)
        return c

    def hello_y(t, c):
        pl.semaphore_signal(bar, inc=1, device_id=(zh * 8 + (y + t) % 8, s), device_id_type=MESH)
        return c

    def act_copy(g):
        rows = pl.ds(g * GRP, GRP)
        return pltpu.make_async_copy(act_h.at[rows], act.at[rows], in_sem.at[g])

    tabs = [
        pltpu.make_async_copy(h, v, tab_sem.at[i])
        for i, (h, v) in enumerate(
            ((by_h, by), (fz_h, fz), (bq_h, bq), (bx_h, bx), (byt_h, byt), (fzw_h, fzw), (cot_h, cot))
        )
    ]
    own_w = pltpu.make_async_copy(w_h, w_own, w_sem)
    tabs[0].start()
    for g in range(8):
        act_copy(g).start()
    own_w.start()
    for t in tabs[1:]:
        t.start()
    lax.fori_loop(1, 64, hello, 0)
    lax.fori_loop(1, 8, hello_y, 0)

    def lanes(ref, g):
        rows = pl.ds(g * GRP, GRP)
        return jnp.concatenate(
            [ref[rows, x].reshape(GRP * NY, NZ) for x in range(2)], axis=1
        )

    def put_mid(g, res):
        for x in range(2):
            rows = pl.ds(pl.multiple_of(x * 64 + g * GRP, GRP), GRP)
            mid[:, rows, :] = res[:, x * NZ:(x + 1) * NZ].reshape(2 * MY, GRP, NZ)

    def get_mid(g):
        parts = []
        for x in range(2):
            rows = pl.ds(pl.multiple_of(x * 64 + g * GRP, GRP), GRP)
            parts.append(mid[:, rows, :].reshape(2 * MY * GRP, NZ).astype(BF16))
        return jnp.concatenate(parts, axis=1)

    def z_and_send(table, sbuf, st):
        for bt in range(4):
            for u in range(4):
                j = (s + 1 + bt * 4 + u) % 16
                pair = jnp.concatenate([mid[2 * j].astype(BF16), mid[2 * j + 1].astype(BF16)], axis=1)
                res = dot(table[...], pair, ((1,), (1,)))
                sbuf[pl.ds(j * 4, 4)] = res.astype(BF16).reshape(4, 4, 128)

            def one(n, c):
                j = (s + 1 + bt * 4 + n // 4) % 16
                z = (zh + 1 + n % 4) % 4
                pltpu.make_async_remote_copy(
                    sbuf.at[j * 4 + z], land.at[st, me], ssem.at[st], rsem.at[st],
                    device_id=(z * 8 + y, j), device_id_type=MESH,
                ).start()
                return c

            lax.fori_loop(0, 16 if bt < 3 else 15, one, 0)
        pltpu.make_async_copy(sbuf.at[s * 4 + zh], land.at[st, me], rsem.at[st]).start()

    def send_back(sbuf, st):
        def one(t, c):
            tt = (me + t) % 64
            pltpu.make_async_remote_copy(
                sbuf.at[tt], land.at[st, s * 4 + zh], ssem.at[st], rsem.at[st],
                device_id=at(tt), device_id_type=MESH,
            ).start()
            return c

        lax.fori_loop(1, 64, one, 0)
        pltpu.make_async_copy(sbuf.at[me], land.at[st, s * 4 + zh], rsem.at[st]).start()

    def landed(st):
        whole = land.at[st]
        pltpu.make_async_copy(whole, whole, rsem.at[st]).wait()

    def share(src, dst, k):
        def one(t, c):
            yy = (y + t) % 8
            pltpu.make_async_remote_copy(
                src.at[yy], dst.at[y], xssem.at[k], xrsem.at[k],
                device_id=(zh * 8 + yy, s), device_id_type=MESH,
            ).start()
            return c

        lax.fori_loop(1, 8, one, 0)
        pltpu.make_async_copy(src.at[y], dst.at[y], xrsem.at[k]).start()

    def to_modes(st, scale):
        r = dot(bq[...], land[st].reshape(256, 128))
        first = jnp.where(low, r[0:128], r[384:512])
        second = jnp.where(low, r[128:256], r[256:384])
        return ((first + pltpu.roll(second, 64, 1)) * scale).astype(BF16)

    def from_modes(mixed, scale):
        r = dot(bx[...], mixed)
        first = jnp.where(low, r[0:256], r[768:1024])
        second = jnp.where(low, r[512:768], r[256:512])
        return ((first + pltpu.roll(second, 64, 1)) * scale).astype(BF16)

    def inverse_z(st, table):
        rows = land[st].reshape(256, 128)
        for j in range(16):
            res = dot(rows[16 * j:16 * (j + 1)], table[...], ((0,), (0,)))
            mid[2 * j] = res[:, :NZ]
            mid[2 * j + 1] = res[:, NZ:]

    which = (lax.broadcasted_iota(jnp.int32, (16, 1), 0) // 4)

    def kron_of(dims):
        rep = (
            lax.broadcasted_iota(jnp.int32, (1024, 64), 0) // 16
            == lax.broadcasted_iota(jnp.int32, (1024, 64), 1)
        ).astype(F32).astype(BF16)
        half = dot(rep, pw_ref[...], dims).astype(BF16)
        for m in range(4):
            full = dot(half[256 * m:256 * (m + 1)], rep, ((1,), (1,)))
            same = (
                lax.broadcasted_iota(jnp.int32, (256, 1024), 0) % 16
                == lax.broadcasted_iota(jnp.int32, (256, 1024), 1) % 16
            )
            kron[256 * m:256 * (m + 1), :] = jnp.where(same, full, 0.0).astype(BF16)

    def pointwise(src, with_offset):
        def step(n, c):
            yb, m = n // 4, n % 4
            rows = pl.ds(pl.multiple_of(yb * 16, 16), 16)
            rhs = jnp.concatenate([src[:, x, rows, :].reshape(1024, NZ) for x in range(2)], axis=1)
            res = dot(kron[pl.ds(pl.multiple_of(m * 256, 256), 256), :], rhs)
            for x in range(2):
                part = res[:, x * NZ:(x + 1) * NZ].reshape(16, 2, 8, NZ)
                if with_offset:
                    part = part + offb[pl.ds(m * 16, 16)][:, None]
                loc[pl.ds(m * 16, 16), x, rows, :] = part.reshape(16, 16, NZ)
            return c

        lax.fori_loop(0, 12, step, 0)

    tabs[0].wait()

    def forward(g, c):
        act_copy(g).wait()
        put_mid(g, dot(by[...], lanes(act, g)))
        return c

    lax.fori_loop(0, 8, forward, 0)
    own_w.wait()
    tabs[1].wait()
    pl.semaphore_wait(bar, 70)

    def send_w(t, c):
        pltpu.make_async_remote_copy(
            w_own, wbuf.at[y], wssem, wrsem, device_id=(zh * 8 + (y + t) % 8, s), device_id_type=MESH
        ).start()
        return c

    z_and_send(fz, send.at[0], 0)
    lax.fori_loop(1, 8, send_w, 0)
    pltpu.make_async_copy(w_own, wbuf.at[y], wrsem).start()

    for t in tabs[2:]:
        t.wait()

    def spread(o, c):
        offb[o] = jnp.full((8, NZ), off_ref[o], F32)
        return c

    lax.fori_loop(0, C, spread, 0)
    kron_of(((1,), (1,)))

    pltpu.make_async_copy(wbuf, wbuf, wrsem).wait()

    def widen(n, c):
        w = wbuf[n // 4, n % 4]
        wf = w.astype(F32)
        turned = pltpu.roll(wf, 64, 1)
        wall[n, 0:64, :] = w
        wall[n, 64:128, :] = jnp.where(low, -turned, turned).astype(BF16)
        return c

    lax.fori_loop(0, 32, widen, 0)

    landed(0)
    spec_in = to_modes(0, 1.0)
    spec[0] = spec_in.reshape(8, 16, 128)
    share(spec.at[0], xin, 0)
    mixed = []
    for t in range(8):
        x = spec_in[16 * t:16 * (t + 1)].astype(F32)
        x4 = jnp.concatenate([jnp.where(which == i, x, 0.0) for i in range(4)], axis=1).astype(BF16)
        mixed.append(dot(x4, wall[4 * t:4 * (t + 1)].reshape(512, 128)))
    mixed = jnp.concatenate(mixed, axis=0).astype(BF16)
    back[0] = from_modes(mixed, 1.0 / (NX * NY * NZ)).reshape(64, 4, 128)
    send_back(back.at[0], 1)
    pointwise(act, True)

    landed(1)
    inverse_z(1, fzw)

    def middle(g, c):
        rows = pl.ds(g * GRP, GRP)
        field = dot(byt[...], get_mid(g))
        halves = []
        for x in range(2):
            value = field[:, x * NZ:(x + 1) * NZ].reshape(GRP, NY, NZ) + loc[rows, x]
            grad = (cot[rows, x].astype(F32) * gelu_slope(value)).astype(BF16)
            slope[rows, x] = grad
            halves.append(grad.reshape(GRP * NY, NZ))
        put_mid(g, dot(by[...], jnp.concatenate(halves, axis=1)))
        return c

    lax.fori_loop(0, 8, middle, 0)
    z_and_send(fzw, send.at[1], 2)
    kron_of(((1,), (0,)))

    landed(2)
    spec_grad = to_modes(2, 1.0 / (NX * NY * NZ))
    spec[1] = spec_grad.reshape(8, 16, 128)
    share(spec.at[1], din, 1)
    mixed = []
    for t in range(8):
        res = dot(spec_grad[16 * t:16 * (t + 1)], wall[4 * t:4 * (t + 1)].reshape(512, 128), ((1,), (1,)))
        total = jnp.where(which == 0, res[:, 0:128], 0.0)
        for i in range(1, 4):
            total = total + jnp.where(which == i, res[:, 128 * i:128 * (i + 1)], 0.0)
        mixed.append(total)
    mixed = jnp.concatenate(mixed, axis=0).astype(BF16)
    back[1] = from_modes(mixed, 1.0).reshape(64, 4, 128)
    send_back(back.at[1], 3)
    pointwise(slope, False)

    for k, buf in enumerate((xin, din)):
        pltpu.make_async_copy(buf, buf, xrsem.at[k]).wait()
    left = xin[...].reshape(128, 128).astype(F32)
    right = din[...].reshape(128, 128)
    mode = lax.broadcasted_iota(jnp.int32, (128, 1), 0) // 4 % 4
    for i in range(4):
        g = dot(jnp.where(mode == i, left, 0.0).astype(BF16), right, ((0,), (0,)))
        turned = pltpu.roll(g[64:128], 64, 1)
        gsb[i] = g[0:64] + jnp.where(low, turned, -turned)
    gs_out = pltpu.make_async_copy(gsb, gs_h, w_sem)
    gs_out.start()

    landed(3)
    inverse_z(3, fz)

    def last(g, c):
        rows = pl.ds(g * GRP, GRP)
        field = dot(byt[...], get_mid(g))
        for x in range(2):
            value = field[:, x * NZ:(x + 1) * NZ].reshape(GRP, NY, NZ) + loc[rows, x]
            outb[rows, x] = value.astype(BF16)
        pltpu.make_async_copy(outb.at[rows], out_h.at[rows], out_sem.at[g]).start()
        return c

    lax.fori_loop(0, 8, last, 0)
    for g in range(8):
        rows = pl.ds(g * GRP, GRP)
        pltpu.make_async_copy(outb.at[rows], out_h.at[rows], out_sem.at[g]).wait()
    gs_out.wait()
    for st in range(4):
        sent = land.at[st, pl.ds(0, 63)]
        pltpu.make_async_copy(sent, sent, ssem.at[st]).wait()
    sent = wbuf.at[pl.ds(0, 7)]
    pltpu.make_async_copy(sent, sent, wssem).wait()
    for k in range(2):
        sent = xin.at[pl.ds(0, 7)]
        pltpu.make_async_copy(sent, sent, xssem.at[k]).wait()


def body(activations, cotangent, mode_weights, pointwise, offsets):
    shape = (C, 2, NY, NZ)
    consts = [jnp.asarray(t) for t in tables()]
    hbm = pl.BlockSpec(memory_space=pl.ANY)
    grad_in, grad_spectral = pl.pallas_call(
        kernel,
        out_shape=(
            jax.ShapeDtypeStruct(shape, BF16),
            jax.ShapeDtypeStruct((4, C, 2 * C), F32),
        ),
        in_specs=[hbm, hbm, hbm, pl.BlockSpec(memory_space=pltpu.VMEM), pl.BlockSpec(memory_space=pltpu.SMEM)]
        + [hbm] * 6,
        out_specs=(hbm, hbm),
        scratch_shapes=[
            pltpu.VMEM(shape, BF16),
            pltpu.VMEM(shape, BF16),
            pltpu.VMEM((4, C, 2 * C), BF16),
        ]
        + [pltpu.VMEM(t.shape, BF16) for t in consts]
        + [
            pltpu.VMEM((2 * MY, 128, NZ), F32),
            pltpu.VMEM(shape, F32),
            pltpu.VMEM(shape, BF16),
            pltpu.VMEM(shape, BF16),
            pltpu.VMEM((C, 8, NZ), F32),
            pltpu.VMEM((1024, 1024), BF16),
            pltpu.VMEM((32, 128, 128), BF16),
            pltpu.VMEM((8, 4, C, 2 * C), BF16),
            pltpu.VMEM((2, 8, 16, 128), BF16),
            pltpu.VMEM((8, 16, 128), BF16),
            pltpu.VMEM((8, 16, 128), BF16),
            pltpu.VMEM((4, C, 2 * C), F32),
            pltpu.VMEM((2, 64, 4, 128), BF16),
            pltpu.VMEM((2, 64, 4, 128), BF16),
            pltpu.VMEM((4, 64, 4, 128), BF16),
            pltpu.SemaphoreType.DMA((8,)),
            pltpu.SemaphoreType.DMA((7,)),
            pltpu.SemaphoreType.DMA,
            pltpu.SemaphoreType.DMA((8,)),
            pltpu.SemaphoreType.DMA((4,)),
            pltpu.SemaphoreType.DMA((4,)),
            pltpu.SemaphoreType.DMA,
            pltpu.SemaphoreType.DMA,
            pltpu.SemaphoreType.DMA((2,)),
            pltpu.SemaphoreType.DMA((2,)),
        ],
        compiler_params=pltpu.CompilerParams(
            collective_id=0, has_side_effects=True, vmem_limit_bytes=48 << 20
        ),
    )(activations.reshape(shape), cotangent.reshape(shape), mode_weights, pointwise, offsets, *consts)
    return grad_in.reshape(activations.shape), grad_spectral


def solution(mesh):
    return jax.shard_map(
        body,
        mesh=mesh,
        in_specs=(
            P("dp", None, "space", None, None),
            P("dp", None, "space", None, None),
            P(("space", "dp"), None, None),
            P(),
            P(),
        ),
        out_specs=(P("dp", None, "space", None, None), P(("space", "dp"), None, None)),
        check_vma=False,
    )
```

time: 176 us -> 85 us (0.48)
  Pallas kernels: 0 us -> 71.9 us
  starting transfers between devices: 51.9 us -> 0 us
  waiting for transfers between devices: 51.9 us -> 0 us
  other arithmetic: 21.8 us -> 0 us
  matrix products: 20.7 us -> 0 us
  local copies, waits for them, and re-layouts: 28.1 us -> 12 us
    pallas_call x0 -> x1, Pallas kernels: none -> 71.9 us  [body(): pl.pallas_call(kernel, out_shape=(jax.ShapeDtypeStruct(shape, BF16), jax....]
    all_to_all x8 -> x0, waiting for transfers between devices: 51.9 us -> none  [the longest x2 19.6 us: to_owners(): lax.all_to_all(spectra, 'dp', split_axis=0, concat_axis=1, tiled=True)]
    all_to_all x8 -> x0, starting transfers between devices: 51.9 us -> none  [the longest x2 17.3 us: to_owners(): lax.all_to_all(spectra, 'dp', split_axis=0, concat_axis=1, tiled=True)]
    dot_general x16 -> x0, matrix products: 20.7 us -> none  [the longest x1 7 us: body(): spectral = jnp.dot(returned, plane_inv, preferred_element_type=jnp.float32)]
    another operation x8 -> x0, other arithmetic: 19.2 us -> none
    convert_element_type x9 -> x0, local copies, waits for them, and re-layouts: 8.06 us -> none  [the longest x1 2.88 us: body(): upstream = cotangent.reshape(flat.shape).astype(jnp.float32)]
    another operation x3 -> x0, local copies, waits for them, and re-layouts: 5.51 us -> none
    reshape x7 -> x0, local copies, waits for them, and re-layouts: 2.43 us -> none  [the longest x2 0.93 us: to_slab(): spectra.reshape(local, modes_x, samples, 2, channels)]
  transfers between devices with their start and end apart: 8 -> 0, of which waited for: 8 -> 0; matrix products, arithmetic and copies ran while one was open for 9% -> 0% of each run, Pallas kernels for 0% -> 0%
where the time goes in v1:
time: 85 us; the launch traced here: 84.6 us
  Pallas kernels  71.9 us (85%)
  local copies, waits for them, and re-layouts  12 us (14%)
    pallas_call x1, Pallas kernels, body(): pl.pallas_call(kernel, out_shape=(jax.ShapeDtypeStruct(shape, BF16), jax....  71.9 us
    unnamed x24, local copies, waits for them, and re-layouts  12 us

profile of v1, /device:TPU:1, one launch (start us, length us, event | category | flops | bytes accessed | tf_op | source)
XLA Modules:
  0.0 84.6 jit_solution(14423615305681355844)
XLA Ops:
  0.6 0.0 copy-start
  0.6 1.4 %copy-done = bf16[1,64,2,48,128]{4,3,2,1,0:T(8,128)(2,1)S(1)} copy-done((bf16[1,64,2,48,128]{4,3,2,1,0:T(8,128)(2,1)S(1)}, bf16[1,64,2,48,128]{4,3,2,1,0:T(8,128)(2,1)}, u32[]{:S(2)}) %copy-start) | copy-done | bytes 1572888
  2.0 0.0 copy-start.1
  2.0 1.4 %copy-done.1 = bf16[1,64,2,48,128]{4,3,2,1,0:T(8,128)(2,1)S(1)} copy-done((bf16[1,64,2,48,128]{4,3,2,1,0:T(8,128)(2,1)S(1)}, bf16[1,64,2,48,128]{4,3,2,1,0:T(8,128)(2,1)}, u32[]{:S(2)}) %copy-start.1) | copy-done | bytes 1572888
  3.4 0.0 copy-start.2
  3.5 0.9 %copy-done.2 = bf16[1024,128]{1,0:T(8,128)(2,1)S(1)} copy-done((bf16[1024,128]{1,0:T(8,128)(2,1)S(1)}, bf16[1024,128]{1,0:T(8,128)(2,1)}, u32[]{:S(2)}) %copy-start.2) | copy-done | bytes 262168
  4.4 0.0 copy-start.3
  4.4 0.9 %copy-done.3 = bf16[512,256]{1,0:T(8,128)(2,1)S(1)} copy-done((bf16[512,256]{1,0:T(8,128)(2,1)S(1)}, bf16[512,256]{1,0:T(8,128)(2,1)}, u32[]{:S(2)}) %copy-start.3) | copy-done | bytes 262168
  5.3 0.0 copy-start.4
  5.4 0.9 %copy-done.4 = bf16[384,256]{1,0:T(8,128)(2,1)S(1)} copy-done((bf16[384,256]{1,0:T(8,128)(2,1)S(1)}, bf16[384,256]{1,0:T(8,128)(2,1)}, u32[]{:S(2)}) %copy-start.4) | copy-done | bytes 196632
  6.3 0.0 copy-start.5
  6.3 0.9 %copy-done.5 = bf16[256,384]{1,0:T(8,128)(2,1)S(1)} copy-done((bf16[256,384]{1,0:T(8,128)(2,1)S(1)}, bf16[256,384]{1,0:T(8,128)(2,1)}, u32[]{:S(2)}) %copy-start.5) | copy-done | bytes 196632
  7.2 0.0 copy-start.6
  7.2 0.8 copy-done.6
  8.0 0.0 copy-start.7
  8.0 0.7 copy-done.7
  8.8 0.0 copy-start.8
  8.8 0.7 copy-done.8
  9.5 0.0 copy-start.9
  9.5 0.7 copy-done.9
  10.2 0.0 copy-start.10
  10.2 0.7 copy-done.10
  10.8 71.9 %shard_map.122 = (bf16[64,2,48,128]{3,2,1,0:T(8,128)(2,1)S(1)}, f32[4,64,128]{2,1,0:T(8,128)S(1)}) custom-call(bf16[64,2,48,128]{3,2,1,0:T(8,128)(2,1)S(1)} %bitcast.3, bf16[64,2,48,128]{3,2,1,0:T(8,128)(2,1)S(1)} %bitcast.4, bf16[4,64,128]{2,1,0:T(8,128)(2,1)S(1)} %copy-done.6, bf16[64,64]{1,0:T(8,128)(2,1)S(1)} %copy-done.7, f32[64]{0:T(128)S(1)} %copy-done.10, ...), custom_call_target="tpu_custom_call" | custom-call | tf_op jit(solution)/shard_map/pallas_call | solution.py:354
  82.8 1.1 %copy.15 = bf16[1,64,2,48,128]{4,3,2,1,0:T(8,128)(2,1)} copy(bf16[1,64,2,48,128]{4,3,2,1,0:T(8,128)(2,1)S(1)} %bitcast.5) | data formatting | bytes 3145728
  83.9 0.7 copy.16
Async XLA Ops:
  0.6 1.4 %copy-start = (bf16[1,64,2,48,128]{4,3,2,1,0:T(8,128)(2,1)S(1)}, bf16[1,64,2,48,128]{4,3,2,1,0:T(8,128)(2,1)}, u32[]{:S(2)}) copy-start(bf16[1,64,2,48,128]{4,3,2,1,0:T(8,128)(2,1)} %param.11) | copy-start | bytes 4718596
  2.0 1.4 %copy-start.1 = (bf16[1,64,2,48,128]{4,3,2,1,0:T(8,128)(2,1)S(1)}, bf16[1,64,2,48,128]{4,3,2,1,0:T(8,128)(2,1)}, u32[]{:S(2)}) copy-start(bf16[1,64,2,48,128]{4,3,2,1,0:T(8,128)(2,1)} %param.12) | copy-start | bytes 4718596
  3.4 0.9 %copy-start.2 = (bf16[1024,128]{1,0:T(8,128)(2,1)S(1)}, bf16[1024,128]{1,0:T(8,128)(2,1)}, u32[]{:S(2)}) copy-start(bf16[1024,128]{1,0:T(8,128)(2,1)} %constant.17.clone.bx_h) | copy-start | bytes 786436
  4.4 0.9 %copy-start.3 = (bf16[512,256]{1,0:T(8,128)(2,1)S(1)}, bf16[512,256]{1,0:T(8,128)(2,1)}, u32[]{:S(2)}) copy-start(bf16[512,256]{1,0:T(8,128)(2,1)} %constant.16.clone.bq_h) | copy-start | bytes 786436
  5.3 0.9 %copy-start.4 = (bf16[384,256]{1,0:T(8,128)(2,1)S(1)}, bf16[384,256]{1,0:T(8,128)(2,1)}, u32[]{:S(2)}) copy-start(bf16[384,256]{1,0:T(8,128)(2,1)} %constant.13.clone.byt_h) | copy-start | bytes 589828
  6.3 0.9 %copy-start.5 = (bf16[256,384]{1,0:T(8,128)(2,1)S(1)}, bf16[256,384]{1,0:T(8,128)(2,1)}, u32[]{:S(2)}) copy-start(bf16[256,384]{1,0:T(8,128)(2,1)} %constant.12.clone.by_h) | copy-start | bytes 589828
  7.2 0.8 copy-start.6
  8.0 0.7 copy-start.7
  8.8 0.7 copy-start.8
  9.5 0.7 copy-start.9
  10.2 0.7 copy-start.10

commit v2 on v1

--- a/solution.py
+++ b/solution.py
@@ -56,7 +56,7 @@
     act_h, cot_h, w_h, pw_ref, off_ref, by_h, byt_h, fz_h, fzw_h, bq_h, bx_h,
     out_h, gs_h,
     act, cot, w_own, by, byt, fz, fzw, bq, bx,
-    mid, loc, slope, outb, offb, kron, wall, wbuf, spec, xin, din, gsb,
+    mid, mix, loc, slope, outb, offb, kron, wall, wbuf, spec, xin, din, gsb,
     send, back, land,
     in_sem, tab_sem, w_sem, out_sem, ssem, rsem, wssem, wrsem, xssem, xrsem,
 ):
@@ -66,17 +66,28 @@
     me = zh * 16 + s
     low = lax.broadcasted_iota(jnp.int32, (1, 128), 1) < 64
 
-    def at(tt):
-        return ((tt // 16) * 8 + y, tt % 16)
+    def far_first(k, half):
+        return half + (1 - 2 * (k % 2)) * ((k + 1) // 2)
+
+    z = 2 * zh + s // 2 % 2
+
+    def peer(n):
+        zt = (z + far_first(n // 8, 4)) % 8
+        xt = (s // 4 + far_first(n // 2 % 4, 2)) % 4
+        return zt // 2, xt * 4 + zt % 2 * 2 + (s + 1 + n) % 2
+
+    def peer_y(n):
+        return (y + far_first(n, 4)) % 8
 
     bar = pltpu.get_barrier_semaphore()
 
-    def hello(t, c):
-        pl.semaphore_signal(bar, inc=1, device_id=at((me + t) % 64), device_id_type=MESH)
+    def hello(n, c):
+        zt, st = peer(n)
+        pl.semaphore_signal(bar, inc=1, device_id=(zt * 8 + y, st), device_id_type=MESH)
         return c
 
-    def hello_y(t, c):
-        pl.semaphore_signal(bar, inc=1, device_id=(zh * 8 + (y + t) % 8, s), device_id_type=MESH)
+    def hello_y(n, c):
+        pl.semaphore_signal(bar, inc=1, device_id=(zh * 8 + peer_y(n), s), device_id_type=MESH)
         return c
 
     def act_copy(g):
@@ -96,8 +107,8 @@
     own_w.start()
     for t in tabs[1:]:
         t.start()
-    lax.fori_loop(1, 64, hello, 0)
-    lax.fori_loop(1, 8, hello_y, 0)
+    lax.fori_loop(0, 63, hello, 0)
+    lax.fori_loop(0, 7, hello_y, 0)
 
     def lanes(ref, g):
         rows = pl.ds(g * GRP, GRP)
@@ -107,46 +118,43 @@
 
     def put_mid(g, res):
         for x in range(2):
-            rows = pl.ds(pl.multiple_of(x * 64 + g * GRP, GRP), GRP)
+            rows = pl.ds(x * 64 + g * GRP, GRP)
             mid[:, rows, :] = res[:, x * NZ:(x + 1) * NZ].reshape(2 * MY, GRP, NZ)
 
     def get_mid(g):
         parts = []
         for x in range(2):
-            rows = pl.ds(pl.multiple_of(x * 64 + g * GRP, GRP), GRP)
+            rows = pl.ds(x * 64 + g * GRP, GRP)
             parts.append(mid[:, rows, :].reshape(2 * MY * GRP, NZ).astype(BF16))
         return jnp.concatenate(parts, axis=1)
 
     def z_and_send(table, sbuf, st):
-        for bt in range(4):
-            for u in range(4):
-                j = (s + 1 + bt * 4 + u) % 16
-                pair = jnp.concatenate([mid[2 * j].astype(BF16), mid[2 * j + 1].astype(BF16)], axis=1)
-                res = dot(table[...], pair, ((1,), (1,)))
-                sbuf[pl.ds(j * 4, 4)] = res.astype(BF16).reshape(4, 4, 128)
-
-            def one(n, c):
-                j = (s + 1 + bt * 4 + n // 4) % 16
-                z = (zh + 1 + n % 4) % 4
-                pltpu.make_async_remote_copy(
-                    sbuf.at[j * 4 + z], land.at[st, me], ssem.at[st], rsem.at[st],
-                    device_id=(z * 8 + y, j), device_id_type=MESH,
-                ).start()
-                return c
-
-            lax.fori_loop(0, 16 if bt < 3 else 15, one, 0)
-        pltpu.make_async_copy(sbuf.at[s * 4 + zh], land.at[st, me], rsem.at[st]).start()
-
-    def send_back(sbuf, st):
-        def one(t, c):
-            tt = (me + t) % 64
+        for j in range(16):
+            pair = jnp.concatenate([mid[2 * j].astype(BF16), mid[2 * j + 1].astype(BF16)], axis=1)
+            res = dot(table[...], pair, ((1,), (1,)))
+            sbuf[4 * j:4 * (j + 1)] = res.astype(BF16).reshape(4, 4, 128)
+
+        def one(n, c):
+            zt, xt = peer(n)
             pltpu.make_async_remote_copy(
-                sbuf.at[tt], land.at[st, s * 4 + zh], ssem.at[st], rsem.at[st],
-                device_id=at(tt), device_id_type=MESH,
+                sbuf.at[xt * 4 + zt], land.at[st, me], ssem.at[st], rsem.at[st],
+                device_id=(zt * 8 + y, xt), device_id_type=MESH,
             ).start()
             return c
 
-        lax.fori_loop(1, 64, one, 0)
+        lax.fori_loop(0, 63, one, 0)
+        pltpu.make_async_copy(sbuf.at[s * 4 + zh], land.at[st, me], rsem.at[st]).start()
+
+    def send_back(sbuf, st):
+        def one(n, c):
+            zt, xt = peer(n)
+            pltpu.make_async_remote_copy(
+                sbuf.at[zt * 16 + xt], land.at[st, s * 4 + zh], ssem.at[st], rsem.at[st],
+                device_id=(zt * 8 + y, xt), device_id_type=MESH,
+            ).start()
+            return c
+
+        lax.fori_loop(0, 63, one, 0)
         pltpu.make_async_copy(sbuf.at[me], land.at[st, s * 4 + zh], rsem.at[st]).start()
 
     def landed(st):
@@ -154,15 +162,15 @@
         pltpu.make_async_copy(whole, whole, rsem.at[st]).wait()
 
     def share(src, dst, k):
-        def one(t, c):
-            yy = (y + t) % 8
+        def one(n, c):
+            yy = peer_y(n)
             pltpu.make_async_remote_copy(
                 src.at[yy], dst.at[y], xssem.at[k], xrsem.at[k],
                 device_id=(zh * 8 + yy, s), device_id_type=MESH,
             ).start()
             return c
 
-        lax.fori_loop(1, 8, one, 0)
+        lax.fori_loop(0, 7, one, 0)
         pltpu.make_async_copy(src.at[y], dst.at[y], xrsem.at[k]).start()
 
     def to_modes(st, scale):
@@ -217,25 +225,31 @@
 
     tabs[0].wait()
 
-    def forward(g, c):
+    def forward(g):
         act_copy(g).wait()
         put_mid(g, dot(by[...], lanes(act, g)))
-        return c
-
-    lax.fori_loop(0, 8, forward, 0)
+
+    for g in range(8):
+        forward(g)
     own_w.wait()
     tabs[1].wait()
     pl.semaphore_wait(bar, 70)
 
-    def send_w(t, c):
+    def weights_to(src, owner, half, step):
         pltpu.make_async_remote_copy(
-            w_own, wbuf.at[y], wssem, wrsem, device_id=(zh * 8 + (y + t) % 8, s), device_id_type=MESH
+            src.at[pl.ds(2 * half, 2)], wbuf.at[owner, pl.ds(2 * half, 2)], wssem, wrsem.at[owner, half],
+            device_id=(zh * 8 + (y + step) % 8, s), device_id_type=MESH,
         ).start()
-        return c
-
+
+    def weights_here(owner, half):
+        here = wbuf.at[owner, pl.ds(2 * half, 2)]
+        pltpu.make_async_copy(here, here, wrsem.at[owner, half]).wait()
+
+    for step in (2, 1):
+        for half in range(2):
+            weights_to(w_own, y, half, step % 8)
+            weights_to(w_own, y, 1 - half, -step % 8)
     z_and_send(fz, send.at[0], 0)
-    lax.fori_loop(1, 8, send_w, 0)
-    pltpu.make_async_copy(w_own, wbuf.at[y], wrsem).start()
 
     for t in tabs[2:]:
         t.wait()
@@ -247,28 +261,35 @@
     lax.fori_loop(0, C, spread, 0)
     kron_of(((1,), (1,)))
 
-    pltpu.make_async_copy(wbuf, wbuf, wrsem).wait()
-
-    def widen(n, c):
-        w = wbuf[n // 4, n % 4]
-        wf = w.astype(F32)
-        turned = pltpu.roll(wf, 64, 1)
-        wall[n, 0:64, :] = w
-        wall[n, 64:128, :] = jnp.where(low, -turned, turned).astype(BF16)
-        return c
-
-    lax.fori_loop(0, 32, widen, 0)
+    before, behind = (y + 6) % 8, (y + 2) % 8
+    for half in range(2):
+        weights_here(before, half)
+        weights_to(wbuf.at[before], before, half, 1)
+        if half == 0:
+            weights_to(wbuf.at[before], before, half, 2)
+        weights_here(behind, 1 - half)
+        weights_to(wbuf.at[behind], behind, 1 - half, 7)
+        if half == 0:
+            weights_to(wbuf.at[behind], behind, 1 - half, 6)
 
     landed(0)
-    spec_in = to_modes(0, 1.0)
-    spec[0] = spec_in.reshape(8, 16, 128)
+    spec[0] = to_modes(0, 1.0).reshape(8, 16, 128)
     share(spec.at[0], xin, 0)
-    mixed = []
-    for t in range(8):
-        x = spec_in[16 * t:16 * (t + 1)].astype(F32)
+
+    for n in range(8):
+        yy = peer_y(7 - n)
+        if n not in (0, 3, 4):
+            weights_here(yy, 0)
+            weights_here(yy, 1)
+        w = (w_own if n == 0 else wbuf.at[yy])[...].reshape(4 * C, 2 * C)
+        turned = pltpu.roll(w.astype(F32), 64, 1)
+        rows = pl.ds(yy * 4, 4)
+        wall[rows, 0:64, :] = w.reshape(4, C, 2 * C)
+        wall[rows, 64:128, :] = jnp.where(low, -turned, turned).astype(BF16).reshape(4, C, 2 * C)
+        x = spec[0, yy].astype(F32)
         x4 = jnp.concatenate([jnp.where(which == i, x, 0.0) for i in range(4)], axis=1).astype(BF16)
-        mixed.append(dot(x4, wall[4 * t:4 * (t + 1)].reshape(512, 128)))
-    mixed = jnp.concatenate(mixed, axis=0).astype(BF16)
+        mix[yy] = dot(x4, wall[rows].reshape(512, 128)).astype(BF16)
+    mixed = mix[...].reshape(128, 128)
     back[0] = from_modes(mixed, 1.0 / (NX * NY * NZ)).reshape(64, 4, 128)
     send_back(back.at[0], 1)
     pointwise(act, True)
@@ -276,7 +297,7 @@
     landed(1)
     inverse_z(1, fzw)
 
-    def middle(g, c):
+    def middle(g):
         rows = pl.ds(g * GRP, GRP)
         field = dot(byt[...], get_mid(g))
         halves = []
@@ -286,9 +307,9 @@
             slope[rows, x] = grad
             halves.append(grad.reshape(GRP * NY, NZ))
         put_mid(g, dot(by[...], jnp.concatenate(halves, axis=1)))
-        return c
-
-    lax.fori_loop(0, 8, middle, 0)
+
+    for g in range(8):
+        middle(g)
     z_and_send(fzw, send.at[1], 2)
     kron_of(((1,), (0,)))
 
@@ -323,16 +344,16 @@
     landed(3)
     inverse_z(3, fz)
 
-    def last(g, c):
+    def last(g):
         rows = pl.ds(g * GRP, GRP)
         field = dot(byt[...], get_mid(g))
         for x in range(2):
             value = field[:, x * NZ:(x + 1) * NZ].reshape(GRP, NY, NZ) + loc[rows, x]
             outb[rows, x] = value.astype(BF16)
         pltpu.make_async_copy(outb.at[rows], out_h.at[rows], out_sem.at[g]).start()
-        return c
-
-    lax.fori_loop(0, 8, last, 0)
+
+    for g in range(8):
+        last(g)
     for g in range(8):
         rows = pl.ds(g * GRP, GRP)
         pltpu.make_async_copy(outb.at[rows], out_h.at[rows], out_sem.at[g]).wait()
@@ -350,7 +371,7 @@
 def body(activations, cotangent, mode_weights, pointwise, offsets):
     shape = (C, 2, NY, NZ)
     consts = [jnp.asarray(t) for t in tables()]
-    hbm = pl.BlockSpec(memory_space=pl.ANY)
+    hbm = pl.BlockSpec(memory_space=pltpu.HBM)
     grad_in, grad_spectral = pl.pallas_call(
         kernel,
         out_shape=(
@@ -368,6 +389,7 @@
         + [pltpu.VMEM(t.shape, BF16) for t in consts]
         + [
             pltpu.VMEM((2 * MY, 128, NZ), F32),
+            pltpu.VMEM((8, 16, 128), BF16),
             pltpu.VMEM(shape, F32),
             pltpu.VMEM(shape, BF16),
             pltpu.VMEM(shape, BF16),
@@ -389,12 +411,12 @@
             pltpu.SemaphoreType.DMA((4,)),
             pltpu.SemaphoreType.DMA((4,)),
             pltpu.SemaphoreType.DMA,
-            pltpu.SemaphoreType.DMA,
+            pltpu.SemaphoreType.DMA((8, 2)),
             pltpu.SemaphoreType.DMA((2,)),
             pltpu.SemaphoreType.DMA((2,)),
         ],
         compiler_params=pltpu.CompilerParams(
-            collective_id=0, has_side_effects=True, vmem_limit_bytes=48 << 20
+            collective_id=0, has_side_effects=True, vmem_limit_bytes=62 << 20
         ),
     )(activations.reshape(shape), cotangent.reshape(shape), mode_weights, pointwise, offsets, *consts)
     return grad_in.reshape(activations.shape), grad_spectral

time: 85 us -> 62 us (0.73)
  Pallas kernels: 71.9 us -> 57.8 us
  local copies, waits for them, and re-layouts: 12 us -> 3.35 us
    pallas_call x1, Pallas kernels: 71.9 us -> 57.8 us  [body(): pl.pallas_call(kernel, out_shape=(jax.ShapeDtypeStruct(shape, BF16), jax....]
    unnamed x24 -> x4, local copies, waits for them, and re-layouts: 12 us -> 3.35 us
where the time goes in v2:
time: 62 us; the launch traced here: 61.8 us
  Pallas kernels  57.8 us (93%)
  local copies, waits for them, and re-layouts  3.35 us (5%)
  between operations  0.65 us (1%)
    pallas_call x1, Pallas kernels, body(): pl.pallas_call(kernel, out_shape=(jax.ShapeDtypeStruct(shape, BF16), jax....  57.8 us
    unnamed x4, local copies, waits for them, and re-layouts  3.35 us

profile of v2, /device:TPU:1, one launch (start us, length us, event | category | flops | bytes accessed | tf_op | source)
XLA Modules:
  0.0 61.8 jit_solution(10200774957378265194)
XLA Ops:
  0.6 57.8 %shard_map.122 = (bf16[64,2,48,128]{3,2,1,0:T(8,128)(2,1)}, f32[4,64,128]{2,1,0:T(8,128)}) custom-call(bf16[64,2,48,128]{3,2,1,0:T(8,128)(2,1)} %bitcast.3, bf16[64,2,48,128]{3,2,1,0:T(8,128)(2,1)} %bitcast.4, bf16[4,64,128]{2,1,0:T(8,128)(2,1)} %w_h.1, bf16[64,64]{1,0:T(8,128)(2,1)} %pw_ref.1, f32[64]{0:T(128)} %off_ref.1, ...), custom_call_target="tpu_custom_call" | custom-call | tf_op jit(solution)/shard_map/pallas_call | solution.py:375
  58.4 0.0 copy-start
  58.5 2.7 %copy.15 = bf16[1,64,2,48,128]{4,3,2,1,0:T(8,128)(2,1)} copy(bf16[1,64,2,48,128]{4,3,2,1,0:T(8,128)(2,1)} %bitcast.5) | data formatting | bytes 3145728
  61.1 0.0 copy-done
  61.1 0.7 %copy.16 = f32[4,64,128]{2,1,0:T(8,128)} copy(f32[4,64,128]{2,1,0:T(8,128)S(1)} %copy-done) | data formatting | bytes 262144
Async XLA Ops:
  58.4 2.7 %copy-start = (f32[4,64,128]{2,1,0:T(8,128)S(1)}, f32[4,64,128]{2,1,0:T(8,128)}, u32[]{:S(2)}) copy-start(f32[4,64,128]{2,1,0:T(8,128)} %get-tuple-element.9) | copy-start | bytes 393220

commit v3 on v2

--- a/solution.py
+++ b/solution.py
@@ -53,9 +53,9 @@
 
 
 def kernel(
-    act_h, cot_h, w_h, pw_ref, off_ref, by_h, byt_h, fz_h, fzw_h, bq_h, bx_h,
+    act_h, cot_h, w_h, pw_h, off_h, by_h, byt_h, fz_h, fzw_h, bq_h, bx_h,
     out_h, gs_h,
-    act, cot, w_own, by, byt, fz, fzw, bq, bx,
+    act, cot, w_own, pw_ref, off_ref, by, byt, fz, fzw, bq, bx,
     mid, mix, loc, slope, outb, offb, kron, wall, wbuf, spec, xin, din, gsb,
     send, back, land,
     in_sem, tab_sem, w_sem, out_sem, ssem, rsem, wssem, wrsem, xssem, xrsem,
@@ -69,26 +69,31 @@
     def far_first(k, half):
         return half + (1 - 2 * (k % 2)) * ((k + 1) // 2)
 
-    z = 2 * zh + s // 2 % 2
+    z = 2 * zh + lax.rem(lax.div(s, 2), 2)
+    zts = [lax.rem(z + k, 8) for k in range(8)]
+    zhs = [lax.div(zt, 2) for zt in zts]
+    xts = [lax.rem(lax.div(s, 4) + k, 4) * 4 for k in range(4)]
+    slabs = [[xt + lax.rem(zt, 2) * 2 for xt in xts] for zt in zts]
+    cores = [lax.rem(s, 2), lax.rem(s + 1, 2)]
+    yys = [lax.rem(y + far_first(k, 4), 8) for k in range(8)]
+    order = sorted(
+        ((dz, dx, dc) for dz in range(8) for dx in range(4) for dc in range(2)),
+        key=lambda d: (-min(d[0], 8 - d[0]) - min(d[1], 4 - d[1]), -d[2]),
+    )
 
     def peer(n):
-        zt = (z + far_first(n // 8, 4)) % 8
-        xt = (s // 4 + far_first(n // 2 % 4, 2)) % 4
-        return zt // 2, xt * 4 + zt % 2 * 2 + (s + 1 + n) % 2
+        dz, dx, dc = order[n]
+        return zhs[dz], slabs[dz][dx] + cores[dc]
 
     def peer_y(n):
-        return (y + far_first(n, 4)) % 8
+        return yys[n]
 
     bar = pltpu.get_barrier_semaphore()
-
-    def hello(n, c):
+    for n in range(63):
         zt, st = peer(n)
         pl.semaphore_signal(bar, inc=1, device_id=(zt * 8 + y, st), device_id_type=MESH)
-        return c
-
-    def hello_y(n, c):
+    for n in range(7):
         pl.semaphore_signal(bar, inc=1, device_id=(zh * 8 + peer_y(n), s), device_id_type=MESH)
-        return c
 
     def act_copy(g):
         rows = pl.ds(g * GRP, GRP)
@@ -97,7 +102,7 @@
     tabs = [
         pltpu.make_async_copy(h, v, tab_sem.at[i])
         for i, (h, v) in enumerate(
-            ((by_h, by), (fz_h, fz), (bq_h, bq), (bx_h, bx), (byt_h, byt), (fzw_h, fzw), (cot_h, cot))
+            ((by_h, by), (fz_h, fz), (bq_h, bq), (bx_h, bx), (byt_h, byt), (fzw_h, fzw), (pw_h, pw_ref), (off_h, off_ref), (cot_h, cot))
         )
     ]
     own_w = pltpu.make_async_copy(w_h, w_own, w_sem)
@@ -107,8 +112,6 @@
     own_w.start()
     for t in tabs[1:]:
         t.start()
-    lax.fori_loop(0, 63, hello, 0)
-    lax.fori_loop(0, 7, hello_y, 0)
 
     def lanes(ref, g):
         rows = pl.ds(g * GRP, GRP)
@@ -128,49 +131,36 @@
             parts.append(mid[:, rows, :].reshape(2 * MY * GRP, NZ).astype(BF16))
         return jnp.concatenate(parts, axis=1)
 
-    def z_and_send(table, sbuf, st):
+    def forward_z(table, sbuf):
         for j in range(16):
             pair = jnp.concatenate([mid[2 * j].astype(BF16), mid[2 * j + 1].astype(BF16)], axis=1)
             res = dot(table[...], pair, ((1,), (1,)))
             sbuf[4 * j:4 * (j + 1)] = res.astype(BF16).reshape(4, 4, 128)
 
-        def one(n, c):
+    def exchange(sbuf, st, to_owner):
+        slot = me if to_owner else s * 4 + zh
+        for n in range(64):
             zt, xt = peer(n)
-            pltpu.make_async_remote_copy(
-                sbuf.at[xt * 4 + zt], land.at[st, me], ssem.at[st], rsem.at[st],
-                device_id=(zt * 8 + y, xt), device_id_type=MESH,
-            ).start()
-            return c
-
-        lax.fori_loop(0, 63, one, 0)
-        pltpu.make_async_copy(sbuf.at[s * 4 + zh], land.at[st, me], rsem.at[st]).start()
-
-    def send_back(sbuf, st):
-        def one(n, c):
-            zt, xt = peer(n)
-            pltpu.make_async_remote_copy(
-                sbuf.at[zt * 16 + xt], land.at[st, s * 4 + zh], ssem.at[st], rsem.at[st],
-                device_id=(zt * 8 + y, xt), device_id_type=MESH,
-            ).start()
-            return c
-
-        lax.fori_loop(0, 63, one, 0)
-        pltpu.make_async_copy(sbuf.at[me], land.at[st, s * 4 + zh], rsem.at[st]).start()
+            block = sbuf.at[xt * 4 + zt] if to_owner else sbuf.at[zt * 16 + xt]
+            if n == 63:
+                pltpu.make_async_copy(block, land.at[st, slot], rsem.at[st]).start()
+            else:
+                pltpu.make_async_remote_copy(
+                    block, land.at[st, slot], ssem.at[st], rsem.at[st],
+                    device_id=(zt * 8 + y, xt), device_id_type=MESH,
+                ).start()
 
     def landed(st):
         whole = land.at[st]
         pltpu.make_async_copy(whole, whole, rsem.at[st]).wait()
 
     def share(src, dst, k):
-        def one(n, c):
+        for n in range(7):
             yy = peer_y(n)
             pltpu.make_async_remote_copy(
                 src.at[yy], dst.at[y], xssem.at[k], xrsem.at[k],
                 device_id=(zh * 8 + yy, s), device_id_type=MESH,
             ).start()
-            return c
-
-        lax.fori_loop(0, 7, one, 0)
         pltpu.make_async_copy(src.at[y], dst.at[y], xrsem.at[k]).start()
 
     def to_modes(st, scale):
@@ -208,7 +198,7 @@
             )
             kron[256 * m:256 * (m + 1), :] = jnp.where(same, full, 0.0).astype(BF16)
 
-    def pointwise(src, with_offset):
+    def pointwise(src, with_offset, parts):
         def step(n, c):
             yb, m = n // 4, n % 4
             rows = pl.ds(pl.multiple_of(yb * 16, 16), 16)
@@ -221,7 +211,7 @@
                 loc[pl.ds(m * 16, 16), x, rows, :] = part.reshape(16, 16, NZ)
             return c
 
-        lax.fori_loop(0, 12, step, 0)
+        lax.fori_loop(4 * parts[0], 4 * parts[1], step, 0)
 
     tabs[0].wait()
 
@@ -233,6 +223,7 @@
         forward(g)
     own_w.wait()
     tabs[1].wait()
+    forward_z(fz, send.at[0])
     pl.semaphore_wait(bar, 70)
 
     def weights_to(src, owner, half, step):
@@ -249,7 +240,7 @@
         for half in range(2):
             weights_to(w_own, y, half, step % 8)
             weights_to(w_own, y, 1 - half, -step % 8)
-    z_and_send(fz, send.at[0], 0)
+    exchange(send.at[0], 0, True)
 
     for t in tabs[2:]:
         t.wait()
@@ -272,6 +263,7 @@
         if half == 0:
             weights_to(wbuf.at[behind], behind, 1 - half, 6)
 
+    pointwise(act, True, (0, 1))
     landed(0)
     spec[0] = to_modes(0, 1.0).reshape(8, 16, 128)
     share(spec.at[0], xin, 0)
@@ -291,8 +283,8 @@
         mix[yy] = dot(x4, wall[rows].reshape(512, 128)).astype(BF16)
     mixed = mix[...].reshape(128, 128)
     back[0] = from_modes(mixed, 1.0 / (NX * NY * NZ)).reshape(64, 4, 128)
-    send_back(back.at[0], 1)
-    pointwise(act, True)
+    exchange(back.at[0], 1, False)
+    pointwise(act, True, (1, 3))
 
     landed(1)
     inverse_z(1, fzw)
@@ -310,8 +302,10 @@
 
     for g in range(8):
         middle(g)
-    z_and_send(fzw, send.at[1], 2)
+    forward_z(fzw, send.at[1])
+    exchange(send.at[1], 2, True)
     kron_of(((1,), (0,)))
+    pointwise(slope, False, (0, 1))
 
     landed(2)
     spec_grad = to_modes(2, 1.0 / (NX * NY * NZ))
@@ -326,8 +320,8 @@
         mixed.append(total)
     mixed = jnp.concatenate(mixed, axis=0).astype(BF16)
     back[1] = from_modes(mixed, 1.0).reshape(64, 4, 128)
-    send_back(back.at[1], 3)
-    pointwise(slope, False)
+    exchange(back.at[1], 3, False)
+    pointwise(slope, False, (1, 3))
 
     for k, buf in enumerate((xin, din)):
         pltpu.make_async_copy(buf, buf, xrsem.at[k]).wait()
@@ -371,6 +365,7 @@
 def body(activations, cotangent, mode_weights, pointwise, offsets):
     shape = (C, 2, NY, NZ)
     consts = [jnp.asarray(t) for t in tables()]
+    operands = (activations.reshape(shape), cotangent.reshape(shape), mode_weights, pointwise, offsets, *consts)
     hbm = pl.BlockSpec(memory_space=pltpu.HBM)
     grad_in, grad_spectral = pl.pallas_call(
         kernel,
@@ -378,13 +373,14 @@
             jax.ShapeDtypeStruct(shape, BF16),
             jax.ShapeDtypeStruct((4, C, 2 * C), F32),
         ),
-        in_specs=[hbm, hbm, hbm, pl.BlockSpec(memory_space=pltpu.VMEM), pl.BlockSpec(memory_space=pltpu.SMEM)]
-        + [hbm] * 6,
-        out_specs=(hbm, hbm),
+        in_specs=[hbm] * 11,
+        out_specs=(pl.BlockSpec(memory_space=pl.ANY),) * 2,
         scratch_shapes=[
             pltpu.VMEM(shape, BF16),
             pltpu.VMEM(shape, BF16),
             pltpu.VMEM((4, C, 2 * C), BF16),
+            pltpu.VMEM((C, C), BF16),
+            pltpu.SMEM((C,), F32),
         ]
         + [pltpu.VMEM(t.shape, BF16) for t in consts]
         + [
@@ -405,7 +401,7 @@
             pltpu.VMEM((2, 64, 4, 128), BF16),
             pltpu.VMEM((4, 64, 4, 128), BF16),
             pltpu.SemaphoreType.DMA((8,)),
-            pltpu.SemaphoreType.DMA((7,)),
+            pltpu.SemaphoreType.DMA((9,)),
             pltpu.SemaphoreType.DMA,
             pltpu.SemaphoreType.DMA((8,)),
             pltpu.SemaphoreType.DMA((4,)),
@@ -416,9 +412,9 @@
             pltpu.SemaphoreType.DMA((2,)),
         ],
         compiler_params=pltpu.CompilerParams(
-            collective_id=0, has_side_effects=True, vmem_limit_bytes=62 << 20
+            collective_id=0, has_side_effects=True, vmem_limit_bytes=32 << 20
         ),
-    )(activations.reshape(shape), cotangent.reshape(shape), mode_weights, pointwise, offsets, *consts)
+    )(*(pltpu.with_memory_space_constraint(a, pltpu.HBM) for a in operands))
     return grad_in.reshape(activations.shape), grad_spectral
 
 

time: 62 us -> 56.3 us (0.908)
  Pallas kernels: 57.8 us -> 53.7 us
  local copies, waits for them, and re-layouts: 3.35 us -> 1.8 us
    pallas_call x1, Pallas kernels: 57.8 us -> 53.7 us  [body(): pl.pallas_call(kernel, out_shape=(jax.ShapeDtypeStruct(shape, BF16), jax....]
    unnamed x4 -> x2, local copies, waits for them, and re-layouts: 3.35 us -> 1.8 us
where the time goes in v3:
time: 56.3 us; the launch traced here: 56.2 us
  Pallas kernels  53.7 us (95%)
  local copies, waits for them, and re-layouts  1.8 us (3%)
  between operations  0.64 us (1%)
    pallas_call x1, Pallas kernels, body(): pl.pallas_call(kernel, out_shape=(jax.ShapeDtypeStruct(shape, BF16), jax....  53.7 us
    unnamed x2, local copies, waits for them, and re-layouts  1.8 us

profile of v3, /device:TPU:1, one launch (start us, length us, event | category | flops | bytes accessed | tf_op | source)
XLA Modules:
  0.0 56.2 jit_solution(13067760827588282137)
XLA Ops:
  0.6 53.7 %shard_map.122 = (bf16[64,2,48,128]{3,2,1,0:T(8,128)(2,1)S(1)}, f32[4,64,128]{2,1,0:T(8,128)S(1)}) custom-call(bf16[64,2,48,128]{3,2,1,0:T(8,128)(2,1)} %bitcast.4, bf16[64,2,48,128]{3,2,1,0:T(8,128)(2,1)} %bitcast.5, bf16[4,64,128]{2,1,0:T(8,128)(2,1)} %w_h.1, bf16[64,64]{1,0:T(8,128)(2,1)} %pw_h.1, f32[64]{0:T(128)} %off_h.1, ...), custom_call_target="tpu_custom_call" | custom-call | tf_op jit(solution)/shard_map/pallas_call | solution.py:370
  54.4 1.1 %copy.15 = bf16[1,64,2,48,128]{4,3,2,1,0:T(8,128)(2,1)} copy(bf16[1,64,2,48,128]{4,3,2,1,0:T(8,128)(2,1)S(1)} %bitcast.3) | data formatting | bytes 3145728
  55.5 0.7 %copy.16 = f32[4,64,128]{2,1,0:T(8,128)} copy(f32[4,64,128]{2,1,0:T(8,128)S(1)} %get-tuple-element.9) | data formatting | bytes 262144

commit v4 on v3

--- a/solution.py
+++ b/solution.py
@@ -37,7 +37,7 @@
     line[:, 1, :, 0], line[:, 1, :, 1] = np.sin(s), np.cos(s)
     line = line.reshape(NX // 2, 2, 2, MX, 2)
     to_q = np.einsum("shuqa,bd,ke->hakqbdseu", line, np.eye(4), np.eye(2)).reshape(512, 256)
-    to_x = np.einsum("shuqa,bd,ke->habskueqd", line, np.eye(4), np.eye(2)).reshape(1024, 128)
+    to_x = np.einsum("shuqa,bd,ke->hbskuaeqd", line, np.eye(4), np.eye(2)).reshape(512, 256)
     cast = lambda t: np.asarray(t.astype(np.float32)).astype(jnp.bfloat16)
     return tuple(cast(t) for t in (to_y, to_y.T.copy(), plain, weighted, to_q, to_x))
 
@@ -52,13 +52,37 @@
     return cdf + value * density
 
 
+def get_mid(mid, g):
+    parts = []
+    for x in range(2):
+        rows = pl.ds(x * 64 + g * GRP, GRP)
+        parts.append(mid[:, rows, :].reshape(2 * MY * GRP, NZ).astype(BF16))
+    return jnp.concatenate(parts, axis=1)
+
+
+def last_kernel(mid, loc, gsb, byt, out_h, gs_h, outb, sem):
+    gs_out = pltpu.make_async_copy(gsb, gs_h, sem.at[8])
+    gs_out.start()
+    copies = []
+    for g in range(8):
+        rows = pl.ds(g * GRP, GRP)
+        field = dot(byt[...], get_mid(mid, g))
+        for x in range(2):
+            value = field[:, x * NZ:(x + 1) * NZ].reshape(GRP, NY, NZ) + loc[rows, x]
+            outb[rows, x] = value.astype(BF16)
+        copies.append(pltpu.make_async_copy(outb.at[rows], out_h.at[rows], sem.at[g]))
+        copies[g].start()
+    for copy in copies + [gs_out]:
+        copy.wait()
+
+
 def kernel(
     act_h, cot_h, w_h, pw_h, off_h, by_h, byt_h, fz_h, fzw_h, bq_h, bx_h,
-    out_h, gs_h,
-    act, cot, w_own, pw_ref, off_ref, by, byt, fz, fzw, bq, bx,
-    mid, mix, loc, slope, outb, offb, kron, wall, wbuf, spec, xin, din, gsb,
+    mid, loc, gsb, byt,
+    act, cot, w_own, pw_ref, off_ref, by, fz, fzw, bq, bx,
+    mix, slope, offb, kron, wall, wbuf, spec, xin, din,
     send, back, land,
-    in_sem, tab_sem, w_sem, out_sem, ssem, rsem, wssem, wrsem, xssem, xrsem,
+    in_sem, tab_sem, w_sem, ssem, rsem, wssem, wrsem, xssem, xrsem,
 ):
     dp = lax.axis_index("dp")
     s = lax.axis_index("space")
@@ -124,13 +148,6 @@
             rows = pl.ds(x * 64 + g * GRP, GRP)
             mid[:, rows, :] = res[:, x * NZ:(x + 1) * NZ].reshape(2 * MY, GRP, NZ)
 
-    def get_mid(g):
-        parts = []
-        for x in range(2):
-            rows = pl.ds(x * 64 + g * GRP, GRP)
-            parts.append(mid[:, rows, :].reshape(2 * MY * GRP, NZ).astype(BF16))
-        return jnp.concatenate(parts, axis=1)
-
     def forward_z(table, sbuf):
         for j in range(16):
             pair = jnp.concatenate([mid[2 * j].astype(BF16), mid[2 * j + 1].astype(BF16)], axis=1)
@@ -169,11 +186,10 @@
         second = jnp.where(low, r[128:256], r[256:384])
         return ((first + pltpu.roll(second, 64, 1)) * scale).astype(BF16)
 
-    def from_modes(mixed, scale):
-        r = dot(bx[...], mixed)
-        first = jnp.where(low, r[0:256], r[768:1024])
-        second = jnp.where(low, r[512:768], r[256:512])
-        return ((first + pltpu.roll(second, 64, 1)) * scale).astype(BF16)
+    def from_modes(mixed, turned, scale):
+        first = dot(bx[0:256], jnp.concatenate([mixed, turned], axis=0))
+        second = dot(bx[256:512], jnp.concatenate([turned, mixed], axis=0))
+        return (jnp.where(low, first, second) * scale).astype(BF16)
 
     def inverse_z(st, table):
         rows = land[st].reshape(256, 128)
@@ -280,9 +296,11 @@
         wall[rows, 64:128, :] = jnp.where(low, -turned, turned).astype(BF16).reshape(4, C, 2 * C)
         x = spec[0, yy].astype(F32)
         x4 = jnp.concatenate([jnp.where(which == i, x, 0.0) for i in range(4)], axis=1).astype(BF16)
-        mix[yy] = dot(x4, wall[rows].reshape(512, 128)).astype(BF16)
-    mixed = mix[...].reshape(128, 128)
-    back[0] = from_modes(mixed, 1.0 / (NX * NY * NZ)).reshape(64, 4, 128)
+        res = dot(x4, wall[rows].reshape(512, 128))
+        mix[0, yy] = res.astype(BF16)
+        mix[1, yy] = pltpu.roll(res, 64, 1).astype(BF16)
+    mixed = [mix[i].reshape(128, 128) for i in range(2)]
+    back[0] = from_modes(*mixed, 1.0 / (NX * NY * NZ)).reshape(64, 4, 128)
     exchange(back.at[0], 1, False)
     pointwise(act, True, (1, 3))
 
@@ -291,7 +309,7 @@
 
     def middle(g):
         rows = pl.ds(g * GRP, GRP)
-        field = dot(byt[...], get_mid(g))
+        field = dot(byt[...], get_mid(mid, g))
         halves = []
         for x in range(2):
             value = field[:, x * NZ:(x + 1) * NZ].reshape(GRP, NY, NZ) + loc[rows, x]
@@ -318,8 +336,9 @@
         for i in range(1, 4):
             total = total + jnp.where(which == i, res[:, 128 * i:128 * (i + 1)], 0.0)
         mixed.append(total)
-    mixed = jnp.concatenate(mixed, axis=0).astype(BF16)
-    back[1] = from_modes(mixed, 1.0).reshape(64, 4, 128)
+    mixed = jnp.concatenate(mixed, axis=0)
+    turned = pltpu.roll(mixed, 64, 1).astype(BF16)
+    back[1] = from_modes(mixed.astype(BF16), turned, 1.0).reshape(64, 4, 128)
     exchange(back.at[1], 3, False)
     pointwise(slope, False, (1, 3))
 
@@ -332,26 +351,9 @@
         g = dot(jnp.where(mode == i, left, 0.0).astype(BF16), right, ((0,), (0,)))
         turned = pltpu.roll(g[64:128], 64, 1)
         gsb[i] = g[0:64] + jnp.where(low, turned, -turned)
-    gs_out = pltpu.make_async_copy(gsb, gs_h, w_sem)
-    gs_out.start()
 
     landed(3)
     inverse_z(3, fz)
-
-    def last(g):
-        rows = pl.ds(g * GRP, GRP)
-        field = dot(byt[...], get_mid(g))
-        for x in range(2):
-            value = field[:, x * NZ:(x + 1) * NZ].reshape(GRP, NY, NZ) + loc[rows, x]
-            outb[rows, x] = value.astype(BF16)
-        pltpu.make_async_copy(outb.at[rows], out_h.at[rows], out_sem.at[g]).start()
-
-    for g in range(8):
-        last(g)
-    for g in range(8):
-        rows = pl.ds(g * GRP, GRP)
-        pltpu.make_async_copy(outb.at[rows], out_h.at[rows], out_sem.at[g]).wait()
-    gs_out.wait()
     for st in range(4):
         sent = land.at[st, pl.ds(0, 63)]
         pltpu.make_async_copy(sent, sent, ssem.at[st]).wait()
@@ -367,14 +369,17 @@
     consts = [jnp.asarray(t) for t in tables()]
     operands = (activations.reshape(shape), cotangent.reshape(shape), mode_weights, pointwise, offsets, *consts)
     hbm = pl.BlockSpec(memory_space=pltpu.HBM)
-    grad_in, grad_spectral = pl.pallas_call(
+    vmem = pl.BlockSpec(memory_space=pltpu.VMEM)
+    handed = pl.pallas_call(
         kernel,
         out_shape=(
-            jax.ShapeDtypeStruct(shape, BF16),
+            jax.ShapeDtypeStruct((2 * MY, 128, NZ), F32),
+            jax.ShapeDtypeStruct(shape, F32),
             jax.ShapeDtypeStruct((4, C, 2 * C), F32),
+            jax.ShapeDtypeStruct(consts[1].shape, BF16),
         ),
         in_specs=[hbm] * 11,
-        out_specs=(pl.BlockSpec(memory_space=pl.ANY),) * 2,
+        out_specs=(vmem,) * 4,
         scratch_shapes=[
             pltpu.VMEM(shape, BF16),
             pltpu.VMEM(shape, BF16),
@@ -382,12 +387,9 @@
             pltpu.VMEM((C, C), BF16),
             pltpu.SMEM((C,), F32),
         ]
-        + [pltpu.VMEM(t.shape, BF16) for t in consts]
+        + [pltpu.VMEM(t.shape, BF16) for t in consts[:1] + consts[2:]]
         + [
-            pltpu.VMEM((2 * MY, 128, NZ), F32),
-            pltpu.VMEM((8, 16, 128), BF16),
-            pltpu.VMEM(shape, F32),
-            pltpu.VMEM(shape, BF16),
+            pltpu.VMEM((2, 8, 16, 128), BF16),
             pltpu.VMEM(shape, BF16),
             pltpu.VMEM((C, 8, NZ), F32),
             pltpu.VMEM((1024, 1024), BF16),
@@ -396,14 +398,12 @@
             pltpu.VMEM((2, 8, 16, 128), BF16),
             pltpu.VMEM((8, 16, 128), BF16),
             pltpu.VMEM((8, 16, 128), BF16),
-            pltpu.VMEM((4, C, 2 * C), F32),
             pltpu.VMEM((2, 64, 4, 128), BF16),
             pltpu.VMEM((2, 64, 4, 128), BF16),
             pltpu.VMEM((4, 64, 4, 128), BF16),
             pltpu.SemaphoreType.DMA((8,)),
             pltpu.SemaphoreType.DMA((9,)),
             pltpu.SemaphoreType.DMA,
-            pltpu.SemaphoreType.DMA((8,)),
             pltpu.SemaphoreType.DMA((4,)),
             pltpu.SemaphoreType.DMA((4,)),
             pltpu.SemaphoreType.DMA,
@@ -415,6 +415,17 @@
             collective_id=0, has_side_effects=True, vmem_limit_bytes=32 << 20
         ),
     )(*(pltpu.with_memory_space_constraint(a, pltpu.HBM) for a in operands))
+    grad_in, grad_spectral = pl.pallas_call(
+        last_kernel,
+        out_shape=(
+            jax.ShapeDtypeStruct(shape, BF16),
+            jax.ShapeDtypeStruct((4, C, 2 * C), F32),
+        ),
+        in_specs=[vmem] * 4,
+        out_specs=(pl.BlockSpec(memory_space=pltpu.HBM),) * 2,
+        scratch_shapes=[pltpu.VMEM(shape, BF16), pltpu.SemaphoreType.DMA((9,))],
+        compiler_params=pltpu.CompilerParams(vmem_limit_bytes=24 << 20),
+    )(*handed)
     return grad_in.reshape(activations.shape), grad_spectral
 
 

time: 56.3 us -> 51.6 us (0.917)
  Pallas kernels: 53.7 us -> 50.9 us
  local copies, waits for them, and re-layouts: 1.8 us -> 0 us
    pallas_call x1 -> x2, Pallas kernels: 53.7 us -> 50.9 us  [the longest x1 49.4 us: body(): pl.pallas_call(kernel, out_shape=(jax.ShapeDtypeStruct((2 * MY, 128, NZ),...]
    unnamed x2 -> x0, local copies, waits for them, and re-layouts: 1.8 us -> none
where the time goes in v4:
time: 51.6 us; the launch traced here: 51.5 us
  Pallas kernels  50.9 us (99%)
  between operations  0.64 us (1%)
    pallas_call x1, Pallas kernels, body(): pl.pallas_call(kernel, out_shape=(jax.ShapeDtypeStruct((2 * MY, 128, NZ),...  49.4 us
    pallas_call x1, Pallas kernels, body(): pl.pallas_call(last_kernel, out_shape=(jax.ShapeDtypeStruct(shape, BF16),...  1.5 us

profile of v4, /device:TPU:1, one launch (start us, length us, event | category | flops | bytes accessed | tf_op | source)
XLA Modules:
  0.0 51.5 jit_solution(2954491272683172942)
XLA Ops:
  0.6 49.4 %shard_map.122 = (f32[32,128,128]{2,1,0:T(8,128)S(1)}, f32[64,2,48,128]{3,2,1,0:T(8,128)S(1)}, f32[4,64,128]{2,1,0:T(8,128)S(1)}, bf16[384,256]{1,0:T(8,128)(2,1)S(1)}) custom-call(bf16[64,2,48,128]{3,2,1,0:T(8,128)(2,1)} %bitcast.3, bf16[64,2,48,128]{3,2,1,0:T(8,128)(2,1)} %bitcast.4, bf16[4,64,128]{2,1,0:T(8,128)(2,1)} %w_h.1, bf16[64,64]{1,0:T(8,128)(2,1)} %pw_h.1, ...), custom_call_target="tpu_custom_call" | custom-call | tf_op jit(solution)/shard_map/pallas_call | solution.py:373
  50.0 1.5 %shard_map.123 = (bf16[64,2,48,128]{3,2,1,0:T(8,128)(2,1)}, f32[4,64,128]{2,1,0:T(8,128)}) custom-call(f32[32,128,128]{2,1,0:T(8,128)S(1)} %get-tuple-element.8.mid, f32[64,2,48,128]{3,2,1,0:T(8,128)S(1)} %get-tuple-element.9.loc, f32[4,64,128]{2,1,0:T(8,128)S(1)} %get-tuple-element.10.gsb, bf16[384,256]{1,0:T(8,128)(2,1)S(1)} %get-tuple-element.11.byt), custom_call_target="tpu_custom_call" | custom-call | tf_op jit(solution)/shard_map/pallas_call | solution.py:418

commit v5 on v4

--- a/solution.py
+++ b/solution.py
@@ -47,9 +47,8 @@
 
 
 def gelu_slope(value):
-    cdf = 0.5 * (1.0 + lax.erf(value * 0.7071067811865476))
-    density = jnp.exp(-0.5 * value * value) * 0.3989422804014327
-    return cdf + value * density
+    density = lax.exp2(value * value * -0.7213475204444817)
+    return 0.5 + (0.5 * lax.erf(value * 0.7071067811865476) + (value * 0.3989422804014327) * density)
 
 
 def get_mid(mid, g):
@@ -328,7 +327,6 @@
     landed(2)
     spec_grad = to_modes(2, 1.0 / (NX * NY * NZ))
     spec[1] = spec_grad.reshape(8, 16, 128)
-    share(spec.at[1], din, 1)
     mixed = []
     for t in range(8):
         res = dot(spec_grad[16 * t:16 * (t + 1)], wall[4 * t:4 * (t + 1)].reshape(512, 128), ((1,), (1,)))
@@ -340,6 +338,7 @@
     turned = pltpu.roll(mixed, 64, 1).astype(BF16)
     back[1] = from_modes(mixed.astype(BF16), turned, 1.0).reshape(64, 4, 128)
     exchange(back.at[1], 3, False)
+    share(spec.at[1], din, 1)
     pointwise(slope, False, (1, 3))
 
     for k, buf in enumerate((xin, din)):

time: 51.6 us -> 51.4 us (level)
  no operation moved by 1% of the time
where the time goes in v5:
time: 51.4 us; the launch traced here: 51.3 us
  Pallas kernels  50.6 us (98%)
  between operations  0.64 us (1%)
    pallas_call x1, Pallas kernels, body(): pl.pallas_call(kernel, out_shape=(jax.ShapeDtypeStruct((2 * MY, 128, NZ),...  49.1 us
    pallas_call x1, Pallas kernels, body(): pl.pallas_call(last_kernel, out_shape=(jax.ShapeDtypeStruct(shape, BF16),...  1.51 us

profile of v5, /device:TPU:1, one launch (start us, length us, event | category | flops | bytes accessed | tf_op | source)
XLA Modules:
  0.0 51.3 jit_solution(6181815645297709798)
XLA Ops:
  0.6 49.1 %shard_map.122 = (f32[32,128,128]{2,1,0:T(8,128)S(1)}, f32[64,2,48,128]{3,2,1,0:T(8,128)S(1)}, f32[4,64,128]{2,1,0:T(8,128)S(1)}, bf16[384,256]{1,0:T(8,128)(2,1)S(1)}) custom-call(bf16[64,2,48,128]{3,2,1,0:T(8,128)(2,1)} %bitcast.3, bf16[64,2,48,128]{3,2,1,0:T(8,128)(2,1)} %bitcast.4, bf16[4,64,128]{2,1,0:T(8,128)(2,1)} %w_h.1, bf16[64,64]{1,0:T(8,128)(2,1)} %pw_h.1, ...), custom_call_target="tpu_custom_call" | custom-call | tf_op jit(solution)/shard_map/pallas_call | solution.py:372
  49.8 1.5 %shard_map.123 = (bf16[64,2,48,128]{3,2,1,0:T(8,128)(2,1)}, f32[4,64,128]{2,1,0:T(8,128)}) custom-call(f32[32,128,128]{2,1,0:T(8,128)S(1)} %get-tuple-element.8.mid, f32[64,2,48,128]{3,2,1,0:T(8,128)S(1)} %get-tuple-element.9.loc, f32[4,64,128]{2,1,0:T(8,128)S(1)} %get-tuple-element.10.gsb, bf16[384,256]{1,0:T(8,128)(2,1)S(1)} %get-tuple-element.11.byt), custom_call_target="tpu_custom_call" | custom-call | tf_op jit(solution)/shard_map/pallas_call | solution.py:417
